TPU v7x, 256 devices: a whole 4x4x8 slice. The times are simulated.
256 devices in a mesh: rows: 64 (over z, x, core), cols: 4 (over y).
Axes of the slice: x: 4, y: 4, z: 8, core: 2. Of those that a mesh axis runs over, the one named last changes fastest.
Arguments:
- pass_rates: float32 [32, 1048576], P(None, 'rows'), may hold values from 0 to 1
- upper_blocks: bfloat16 [8192, 8, 128, 128], P('rows', 'cols'), may hold values from 9.9658966e-05 to 0.0099487305
- neighbours: int32 [8192, 8], P('rows', 'cols'), may hold values from 0 to 8191, as said below
Outputs:
- solution: float32 [32, 1048576], P('cols', 'rows')
- residual: float32 [32, 1048576], P('cols', 'rows')
Inputs may be any that keep to these rules, and one draw needn't show every extreme that they name: `neighbours`: slot 0 of block-row b names b itself; every other slot of block-row b names a block from b to b + 256 that exists; in the last block-row of every shard of 128 block-rows, slot 1 names the farthest such block.
All inputs are finite; a program needn't handle non-finite values.
Results may differ from a plain program's by a relative error of at most 0.034.
Values may be sent and summed in bfloat16 or wider, within the bound.
A program may use at most 128 MiB of HBM per device.

v0:
```python
import jax
import jax.numpy as jnp
from jax import lax
from jax.sharding import PartitionSpec as P

REACH = 2
ITERS = 2


def from_behind(value, axis, steps):
    count = lax.axis_size(axis)
    initial, last = (max(0, -steps), min(count, count - steps))
    return lax.ppermute(value, axis, [(source, source + steps) for source in range(initial, last)])


def per_device(pass_rates, upper_blocks, neighbours):
    shard_rows = upper_blocks.shape[0]
    block_width = upper_blocks.shape[2]
    columns = pass_rates.shape[0]
    first_block = lax.axis_index("rows") * shard_rows
    local_index = neighbours - first_block
    own_weight = jnp.sum(upper_blocks, axis=(1, 3), dtype=jnp.float32)
    col_weight = jnp.sum(upper_blocks, axis=2, dtype=jnp.float32)
    share = columns // lax.axis_size("cols")
    residual = pass_rates

    def squares(values):
        return lax.psum(jnp.sum(values * values, axis=1), "rows")

    solution = jnp.zeros_like(residual)
    direction = residual
    norm_now = squares(residual)
    for iteration in range(ITERS):
        rounded = direction.astype(jnp.bfloat16)
        pieces = [rounded]
        for distance in range(1, REACH + 1):
            pieces.append(from_behind(rounded, "rows", -distance))
        window = jnp.concatenate(pieces, axis=1).reshape(
            columns, (REACH + 1) * shard_rows, block_width
        )
        own_block = rounded.reshape(columns, shard_rows, block_width)
        far_blocks = jnp.take(window, local_index, axis=1)
        forward = own_block.astype(jnp.float32) * own_weight[None] - jnp.einsum(
            "bkij,cbkj->cbi", upper_blocks, far_blocks, preferred_element_type=jnp.float32
        )
        transposed = col_weight[None] * far_blocks.astype(jnp.float32) - jnp.einsum(
            "bkij,cbi->cbkj", upper_blocks, own_block, preferred_element_type=jnp.float32
        )
        returned = jnp.zeros(window.shape, jnp.float32).at[:, local_index].add(transposed)
        summed = forward + returned[:, :shard_rows]
        for distance in range(1, REACH + 1):
            summed = summed + from_behind(
                returned[:, distance * shard_rows : (distance + 1) * shard_rows], "rows", distance
            )
        spread = lax.psum(summed, "cols")
        mapped = direction + 0.5 * spread.reshape(direction.shape)
        step_size = norm_now / lax.psum(jnp.sum(direction * mapped, axis=1), "rows")
        solution = solution + step_size[:, None] * direction
        residual = residual - step_size[:, None] * mapped
        if iteration + 1 < ITERS:
            norm_next = squares(residual)
            direction = residual + (norm_next / norm_now)[:, None] * direction
            norm_now = norm_next
    solution = lax.dynamic_slice_in_dim(solution, lax.axis_index("cols") * share, share, 0)
    residual = lax.dynamic_slice_in_dim(residual, lax.axis_index("cols") * share, share, 0)
    return (solution, residual)


def solution(mesh):
    in_specs = (P(None, "rows"), P("rows", "cols", None, None), P("rows", "cols"))
    out_specs = (P("cols", "rows"), P("cols", "rows"))
    return jax.shard_map(
        per_device, mesh=mesh, in_specs=in_specs, out_specs=out_specs, check_vma=False
    )
```

profile of v0, /device:TPU:6, one launch (start us, length us, event | category | flops | bytes accessed | tf_op | source)
XLA Modules:
  0.0 874.6 jit_solution(16670303994397478807)
XLA Ops:
  7.2 2.8 convert_element_type.22
  15.5 5.8 convert_reduce_fusion.1
  21.4 17.9 %collective-permute-done.1 = bf16[32,16384]{1,0:T(8,128)(2,1)} collective-permute-done((bf16[32,16384]{1,0:T(8,128)(2,1)}, bf16[32,16384]{1,0:T(8,128)(2,1)}, u32[]{:S(2)}, u32[]{:S(2)}) %collective-permute-start.1) | collective-permute-done | bytes 1048608 | tf_op jit(solution)/shard_map/ppermute | solution.py:13
  39.2 7.5 collective-permute-done
  46.7 3.3 copy_bitcast_fusion.1
  50.0 4.0 gather_fusion
  54.0 8.5 bitcast_subtract_fusion.1
  62.6 3.5 broadcast.23.clone
  66.0 33.9 %scatter_fusion = f32[32,384,128]{2,0,1:T(8,128)} fusion(f32[32,384,128]{2,0,1:T(8,128)} %broadcast.23.clone, s32[256]{0:T(256)S(1)} %reshape.76, f32[256,32,128]{2,1,0:T(8,128)} %bitcast.94), kind=kCustom, calls=%fused_computation.2 | custom fusion | flops 1048576 | bytes 12583936 | tf_op jit(solution)/shard_map/scatter-add | solution.py:49
  102.8 5.5 collective-permute-start.2
  110.2 36.6 %collective-permute-done.2 = f32[32,128,128]{2,0,1:T(8,128)S(1)} collective-permute-done((f32[32,128,128]{2,0,1:T(8,128)S(1)}, f32[32,128,128]{2,0,1:T(8,128)S(1)}, u32[]{:S(2)}, u32[]{:S(2)}) %collective-permute-start.2) | collective-permute-done | bytes 2097184 | tf_op jit(solution)/shard_map/ppermute | solution.py:13
  146.8 12.0 %collective-permute-done.3 = f32[32,128,128]{2,0,1:T(8,128)S(1)} collective-permute-done((f32[32,128,128]{2,0,1:T(8,128)S(1)}, f32[32,128,128]{2,0,1:T(8,128)S(1)}, u32[]{:S(2)}, u32[]{:S(2)}) %collective-permute-start.3) | collective-permute-done | bytes 2097184 | tf_op jit(solution)/shard_map/ppermute | solution.py:13
  158.7 8.3 fusion.3
  167.1 85.2 %all-reduce.4.cloned.1.call-done = f32[32,128,128]{2,0,1:T(8,128)} async-done(((f32[32,128,128]{2,0,1:T(8,128)}), f32[32,128,128]{2,0,1:T(8,128)}) %all-reduce.4.cloned.1.call-update) | async-done | bytes 2097168 | tf_op jit(solution)/shard_map/psum | solution.py:55
  254.4 114.1 %all-reduce = (f32[32]{0:T(128)S(1)}, f32[32]{0:T(128)S(1)}) all-reduce(f32[32]{0:T(128)S(1)} %get-tuple-element.6, f32[32]{0:T(128)S(1)} %get-tuple-element.5), channel_id=1, replica_groups=mesh['rows'=64,'cols'=4] {'rows'}, use_global_device_ids=true, to_apply=%region_1.0 | all-reduce | flops 64 | bytes 512 | tf_op jit(solution)/shard_map/psum | solution.py:28
  368.6 3.4 multiply_reduce_fusion.1
  372.0 124.1 %psum.45 = f32[32]{0:T(128)S(1)} all-reduce(f32[32]{0:T(128)S(1)} %get-tuple-element.11), channel_id=1, replica_groups=mesh['rows'=64,'cols'=4] {'rows'}, use_global_device_ids=true, to_apply=%region_9.11 | all-reduce | flops 32 | bytes 256 | tf_op jit(solution)/shard_map/psum | solution.py:28
  496.1 3.3 fusion.19
  499.3 7.5 collective-permute-start.5
  506.8 6.9 collective-permute-start.4
  514.9 14.3 %collective-permute-done.5 = bf16[32,16384]{1,0:T(8,128)(2,1)S(1)} collective-permute-done((bf16[32,16384]{1,0:T(8,128)(2,1)S(1)}, bf16[32,16384]{1,0:T(8,128)(2,1)S(1)}, u32[]{:S(2)}, u32[]{:S(2)}) %collective-permute-start.5) | collective-permute-done | bytes 1048608 | tf_op jit(solution)/shard_map/ppermute | solution.py:13
  529.2 11.2 %collective-permute-done.4 = bf16[32,16384]{1,0:T(8,128)(2,1)S(1)} collective-permute-done((bf16[32,16384]{1,0:T(8,128)(2,1)S(1)}, bf16[32,16384]{1,0:T(8,128)(2,1)S(1)}, u32[]{:S(2)}, u32[]{:S(2)}) %collective-permute-start.4) | collective-permute-done | bytes 1048608 | tf_op jit(solution)/shard_map/ppermute | solution.py:13
  542.4 4.1 gather_fusion.1
  546.5 8.7 bitcast_subtract_fusion
  555.1 3.5 broadcast.23
  558.6 33.9 %scatter_fusion.1 = f32[32,384,128]{2,0,1:T(8,128)} fusion(f32[32,384,128]{2,0,1:T(8,128)} %broadcast.23, s32[256]{0:T(256)S(1)} %reshape.76, f32[256,32,128]{2,1,0:T(8,128)} %bitcast.93), kind=kCustom, calls=%fused_computation.3 | custom fusion | flops 1048576 | bytes 12583936 | tf_op jit(solution)/shard_map/scatter-add | solution.py:49
  599.2 40.1 %collective-permute-done.6 = f32[32,128,128]{2,0,1:T(8,128)S(1)} collective-permute-done((f32[32,128,128]{2,0,1:T(8,128)S(1)}, f32[32,128,128]{2,0,1:T(8,128)S(1)}, u32[]{:S(2)}, u32[]{:S(2)}) %collective-permute-start.6) | collective-permute-done | bytes 2097184 | tf_op jit(solution)/shard_map/ppermute | solution.py:13
  639.4 11.9 %collective-permute-done.7 = f32[32,128,128]{2,0,1:T(8,128)S(1)} collective-permute-done((f32[32,128,128]{2,0,1:T(8,128)S(1)}, f32[32,128,128]{2,0,1:T(8,128)S(1)}, u32[]{:S(2)}, u32[]{:S(2)}) %collective-permute-start.7) | collective-permute-done | bytes 2097184 | tf_op jit(solution)/shard_map/ppermute | solution.py:13
  651.3 8.3 fusion.1
  659.8 87.3 %all-reduce.6.cloned.1.call-done = f32[32,128,128]{2,0,1:T(8,128)} async-done(((f32[32,128,128]{2,0,1:T(8,128)}), f32[32,128,128]{2,0,1:T(8,128)}) %all-reduce.6.cloned.1.call-update) | async-done | bytes 2097168 | tf_op jit(solution)/shard_map/psum | solution.py:55
  747.1 4.0 bitcast_add_fusion
  751.0 114.1 %psum.47 = f32[32]{0:T(128)S(1)} all-reduce(f32[32]{0:T(128)S(1)} %get-tuple-element.20), channel_id=1, replica_groups=mesh['rows'=64,'cols'=4] {'rows'}, use_global_device_ids=true, to_apply=%region_13.15 | all-reduce | flops 32 | bytes 256 | tf_op jit(solution)/shard_map/psum | solution.py:57
  (35 shorter events, 24.8 us)
Async XLA Ops:
  7.2 8.0 copy-start
  7.2 7.5 copy-start.3
  7.2 245.1 %all-reduce.4.cloned.1.call-start = ((), (), s32[]{:S(2)}) async-start(), calls=%async_computation | async-start | bytes 4194304 | tf_op jit(solution)/shard_map/psum | solution.py:55
  10.0 29.2 %collective-permute-start.1 = (bf16[32,16384]{1,0:T(8,128)(2,1)}, bf16[32,16384]{1,0:T(8,128)(2,1)}, u32[]{:S(2)}, u32[]{:S(2)}) collective-permute-start(bf16[32,16384]{1,0:T(8,128)(2,1)} %convert_element_type.22), channel_id=1, source_target_pairs={{8,0},{12,4},{16,8},{20,12},{24,16},{28,20},{32,24},{36,28},{40,32... | collective-permute-start | bytes 3145736 | tf_op jit(solution)/shard_map/ppermute | solution.py:13
  12.8 33.9 %collective-permute-start = (bf16[32,16384]{1,0:T(8,128)(2,1)}, bf16[32,16384]{1,0:T(8,128)(2,1)}, u32[]{:S(2)}, u32[]{:S(2)}) collective-permute-start(bf16[32,16384]{1,0:T(8,128)(2,1)} %convert_element_type.22), channel_id=1, source_target_pairs={{4,0},{8,4},{12,8},{16,12},{20,16},{24,20},{28,24},{32,28},{36,32}... | collective-permute-start | bytes 3145736 | tf_op jit(solution)/shard_map/ppermute | solution.py:13
  100.0 58.8 %copy-start.1 = (bf16[256,32,128]{2,1,0:T(8,128)(2,1)S(1)}, bf16[256,32,128]{2,1,0:T(8,128)(2,1)}, u32[]{:S(2)}) copy-start(bf16[256,32,128]{2,1,0:T(8,128)(2,1)} %gather_fusion) | copy-start | bytes 6291460
  102.8 44.0 %collective-permute-start.2 = (f32[32,128,128]{2,0,1:T(8,128)S(1)}, f32[32,128,128]{2,0,1:T(8,128)S(1)}, u32[]{:S(2)}, u32[]{:S(2)}) collective-permute-start(f32[32,128,128]{2,0,1:T(8,128)S(1)} %get-tuple-element.17), channel_id=1, source_target_pairs={{0,4},{4,8},{8,12},{12,16},{16,20},{20,24},{24,28},{28,32},{32,36}... | collective-permute-start | bytes 6291464 | tf_op jit(solution)/shard_map/ppermute | solution.py:13
  108.3 50.5 %collective-permute-start.3 = (f32[32,128,128]{2,0,1:T(8,128)S(1)}, f32[32,128,128]{2,0,1:T(8,128)S(1)}, u32[]{:S(2)}, u32[]{:S(2)}) collective-permute-start(f32[32,128,128]{2,0,1:T(8,128)S(1)} %get-tuple-element.18), channel_id=1, source_target_pairs={{0,8},{4,12},{8,16},{12,20},{16,24},{20,28},{24,32},{28,36},{32,40... | collective-permute-start | bytes 6291464 | tf_op jit(solution)/shard_map/ppermute | solution.py:13
  167.0 580.0 %all-reduce.6.cloned.1.call-start = ((), (), s32[]{:S(2)}) async-start(), calls=%async_computation.1 | async-start | bytes 4194304 | tf_op jit(solution)/shard_map/psum | solution.py:55
  499.3 29.9 %collective-permute-start.5 = (bf16[32,16384]{1,0:T(8,128)(2,1)S(1)}, bf16[32,16384]{1,0:T(8,128)(2,1)S(1)}, u32[]{:S(2)}, u32[]{:S(2)}) collective-permute-start(bf16[32,16384]{1,0:T(8,128)(2,1)S(1)} %get-tuple-element.9), channel_id=1, source_target_pairs={{8,0},{12,4},{16,8},{20,12},{24,16},{28,20},{32,24},{36,28},{40,32... | collective-permute-start | bytes 3145736 | tf_op jit(solution)/shard_map/ppermute | solution.py:13
  506.8 33.7 %collective-permute-start.4 = (bf16[32,16384]{1,0:T(8,128)(2,1)S(1)}, bf16[32,16384]{1,0:T(8,128)(2,1)S(1)}, u32[]{:S(2)}, u32[]{:S(2)}) collective-permute-start(bf16[32,16384]{1,0:T(8,128)(2,1)S(1)} %get-tuple-element.9), channel_id=1, source_target_pairs={{4,0},{8,4},{12,8},{16,12},{20,16},{24,20},{28,24},{32,28},{36,32}... | collective-permute-start | bytes 3145736 | tf_op jit(solution)/shard_map/ppermute | solution.py:13
  592.5 58.8 %copy-start.2 = (bf16[256,32,128]{2,1,0:T(8,128)(2,1)S(1)}, bf16[256,32,128]{2,1,0:T(8,128)(2,1)}, u32[]{:S(2)}) copy-start(bf16[256,32,128]{2,1,0:T(8,128)(2,1)} %gather_fusion.1) | copy-start | bytes 6291460
  595.4 44.0 %collective-permute-start.6 = (f32[32,128,128]{2,0,1:T(8,128)S(1)}, f32[32,128,128]{2,0,1:T(8,128)S(1)}, u32[]{:S(2)}, u32[]{:S(2)}) collective-permute-start(f32[32,128,128]{2,0,1:T(8,128)S(1)} %get-tuple-element.15), channel_id=1, source_target_pairs={{0,4},{4,8},{8,12},{12,16},{16,20},{20,24},{24,28},{28,32},{32,36}... | collective-permute-start | bytes 6291464 | tf_op jit(solution)/shard_map/ppermute | solution.py:13
  597.3 54.0 %collective-permute-start.7 = (f32[32,128,128]{2,0,1:T(8,128)S(1)}, f32[32,128,128]{2,0,1:T(8,128)S(1)}, u32[]{:S(2)}, u32[]{:S(2)}) collective-permute-start(f32[32,128,128]{2,0,1:T(8,128)S(1)} %get-tuple-element.16), channel_id=1, source_target_pairs={{0,8},{4,12},{8,16},{12,20},{16,24},{20,28},{24,32},{28,36},{32,40... | collective-permute-start | bytes 6291464 | tf_op jit(solution)/shard_map/ppermute | solution.py:13
Sparse Core Ops, SparseCore 0:
  167.2 85.0 all-reduce.3
  659.8 87.2 all-reduce.5
where the time goes:
time: 889 us; the launch traced here: 875 us
  blocking collectives  352 us (40%)
  waiting for transfers between devices  324 us (36%)
  other arithmetic  97.1 us (11%)
  matrix products  33.8 us (4%)
  starting transfers between devices  30.3 us (3%)
  local copies, waits for them, and re-layouts  22.7 us (3%)
  between operations  14.2 us (2%)
    psum x2, blocking collectives, squares(): return lax.psum(jnp.sum(values * values, axis=1), 'rows')  238 us
    psum x2, waiting for transfers between devices, per_device(): spread = lax.psum(summed, 'cols')  173 us
    ppermute x8, waiting for transfers between devices, from_behind(): lax.ppermute(value, axis, [(source, source + steps) for source in range(i...  152 us
    psum x1, blocking collectives, per_device(): step_size = norm_now / lax.psum(jnp.sum(direction * mapped, axis=1), 'rows')  114 us
    scatter-add x2, other arithmetic, per_device(): jnp.zeros(window.shape, jnp.float32).at[:, local_index].add(transposed)  67.9 us
    ppermute x8, starting transfers between devices, from_behind(): lax.ppermute(value, axis, [(source, source + steps) for source in range(i...  30.2 us
  transfers between devices with their start and end apart: 10, of which 10 were waited for; matrix products, arithmetic and copies ran while one was open for 1% of the time, Pallas kernels for 0%

commit v1 on v0

v1 whole, which is shorter than its diff:
```python
import functools

import jax
import jax.numpy as jnp
from jax import lax
from jax.experimental import pallas as pl
from jax.experimental.pallas import tpu as pltpu
from jax.sharding import PartitionSpec as P

MESH = pl.DeviceIdType.MESH
F32 = jnp.float32
BF16 = jnp.bfloat16
RING = 4
VMEM = pl.BlockSpec(memory_space=pltpu.VMEM)
LIMIT = 48 * 2**20
ONES = 16
STEP_ROWS = 8


def rem(value, count):
    return lax.rem(value, jnp.int32(count))


class Place:
    def __init__(self, shards):
        self.shards = shards
        self.s = lax.axis_index("rows")
        self.y = lax.axis_index("cols")
        self.odd = rem(self.s, 2)
        self.next_y = rem(self.y + 1, RING)
        self.last_y = rem(self.y + RING - 1, RING)
        self.far_y = rem(self.y + 2, RING)
        self.partner = (self.s + 1 - 2 * self.odd, self.y)
        self.ahead = (rem(self.s + 2, shards), self.y)
        self.behind = (rem(self.s + shards - 2, shards), self.y)
        self.right = (self.s, self.next_y)
        self.left = (self.s, self.last_y)

    def around(self, stride, size, step):
        at = rem(self.s // stride, size)
        return (self.s + (rem(at + step, size) - at) * stride, self.y)


def signal_all(devices):
    barrier = pltpu.get_barrier_semaphore()
    for device in devices:
        pl.semaphore_signal(barrier, inc=1, device_id=device, device_id_type=MESH)


def wait_all(devices):
    pl.semaphore_wait(pltpu.get_barrier_semaphore(), len(devices))


def remote(src, dst, send_sem, recv_sem, device):
    return pltpu.make_async_remote_copy(
        src_ref=src, dst_ref=dst, send_sem=send_sem, recv_sem=recv_sem, device_id=device, device_id_type=MESH
    )


class Spread:
    def __init__(self, at, plane, send, recv):
        half = plane.shape[1] // 2
        low, high = pl.ds(0, half), pl.ds(half, half)
        routes = (
            (at.y, low, at.right),
            (at.y, high, at.left),
            (at.y, high, at.right),
            (at.y, low, at.left),
            (at.last_y, low, at.right),
            (at.next_y, high, at.left),
        )
        self.copies = [
            remote(plane.at[chunk, part], plane.at[chunk, part], send.at[i], recv.at[i], device)
            for i, (chunk, part, device) in enumerate(routes)
        ]

    def start(self):
        for copy in self.copies[:4]:
            copy.start()

    def relay(self):
        for first, second in ((0, 4), (1, 5)):
            self.copies[first].wait_recv()
            self.copies[second].start()

    def near(self):
        for i in (2, 3):
            self.copies[i].wait_recv()

    def far(self):
        for i in (4, 5):
            self.copies[i].wait_recv()

    def drain(self):
        for copy in self.copies:
            copy.wait_send()


class Gather:
    def __init__(self, at, window, own, send, recv, x_send, x_recv, p_send, p_recv):
        self.at = at
        self.to_behind = remote(window.at[0, at.y], window.at[2, at.y], x_send, x_recv, at.behind)
        self.planes = [Spread(at, window.at[d], send.at[i], recv.at[i]) for i, d in enumerate((0, 2)) if own or d]
        source = 2 - 2 * at.odd
        self.across = [
            remote(window.at[source, chunk], window.at[1, chunk], p_send.at[i], p_recv.at[i], at.partner)
            for i, chunk in enumerate((at.y, at.last_y, at.next_y, at.far_y))
        ]

    def run(self):
        own, ahead = (self.planes[0] if len(self.planes) > 1 else None), self.planes[-1]
        if own is not None:
            own.start()
            own.relay()
        self.to_behind.wait_recv()
        ahead.start()
        self.across[0].start()
        ahead.relay()
        if own is not None:
            own.near()
        ahead.near()
        self.across[1].start()
        self.across[2].start()
        if own is not None:
            own.far()
        ahead.far()
        self.across[3].start()
        for plane in self.planes:
            plane.drain()
        for copy in self.across:
            copy.wait()
        self.to_behind.wait_send()


def halo_kernel(shards, p_ref, window, send, recv, x_send, x_recv, p_send, p_recv):
    at = Place(shards)
    partners = (at.partner, at.ahead, at.behind, at.right, at.left)
    signal_all(partners)
    blocks, columns, width = window.shape[2:]

    def cast(chunk):
        def one(i, carry):
            first = pl.multiple_of((chunk * blocks + i) * width, width)
            window[0, chunk, i] = p_ref[:, pl.ds(first, width)].astype(BF16)
            return carry

        lax.fori_loop(0, blocks, one, 0)

    gather = Gather(at, window, False, send, recv, x_send, x_recv, p_send, p_recv)
    cast(at.y)
    wait_all(partners)
    gather.to_behind.start()
    for chunk in (at.last_y, at.next_y, at.far_y):
        cast(chunk)
    gather.run()


GATHER_SEMS = [
    pltpu.SemaphoreType.DMA((2, 6)),
    pltpu.SemaphoreType.DMA((2, 6)),
    pltpu.SemaphoreType.DMA,
    pltpu.SemaphoreType.DMA,
    pltpu.SemaphoreType.DMA((4,)),
    pltpu.SemaphoreType.DMA((4,)),
]
REDUCE_SEMS = [
    pltpu.SemaphoreType.DMA((4,)),
    pltpu.SemaphoreType.DMA((4,)),
    pltpu.SemaphoreType.DMA((2, 6)),
    pltpu.SemaphoreType.DMA((2, 6)),
    pltpu.SemaphoreType.DMA,
    pltpu.SemaphoreType.DMA,
]


def reduce_scratch(blocks, sub, width):
    return [
        pltpu.VMEM((RING, blocks, sub, width), BF16),
        pltpu.VMEM((2, RING, blocks, sub, width), BF16),
        pltpu.VMEM((2, 6, blocks // 2, sub, width), BF16),
        pltpu.VMEM((blocks, sub, width), BF16),
        pltpu.VMEM((blocks, sub, width), BF16),
    ] + REDUCE_SEMS


class Reduce:
    def __init__(self, at, part, crossed, total, landed, outgoing, incoming, c_send, c_recv, send, recv, x_send, x_recv):
        self.at, self.part, self.crossed, self.total, self.landed = at, part, crossed, total, landed
        self.outgoing, self.incoming = outgoing, incoming
        self.half = crossed.shape[1] // 2
        half = self.half
        self.order = (at.far_y, at.next_y, at.last_y, at.y)
        self.across = [
            remote(part.at[1, chunk], crossed.at[chunk], c_send.at[i], c_recv.at[i], at.partner)
            for i, chunk in enumerate(self.order)
        ]
        low, high = pl.ds(0, half), pl.ds(half, half)
        routes = (
            (at.far_y, low, at.right),
            (at.far_y, high, at.left),
            (at.next_y, high, at.right),
            (at.last_y, low, at.left),
            (at.next_y, low, at.right),
            (at.last_y, high, at.left),
        )
        self.copies = [
            [
                remote(total.at[j, chunk, part_], landed.at[j, i], send.at[j, i], recv.at[j, i], device)
                for i, (chunk, part_, device) in enumerate(routes)
            ]
            for j in range(2)
        ]
        self.to_ahead = remote(outgoing, incoming, x_send, x_recv, at.ahead)

    def start(self):
        for copy in self.across:
            copy.start()

    def combine(self, index):
        at, chunk = self.at, self.order[index]
        joined = 1 - at.odd
        kept = at.odd
        self.across[index].wait_recv()

        def one(i, carry):
            term = self.part[2 * joined, chunk, i].astype(F32) + self.crossed[chunk, i].astype(F32)
            self.total[joined, chunk, i] = term.astype(BF16)
            self.total[kept, chunk, i] = self.part[2 * kept, chunk, i]
            return carry

        lax.fori_loop(0, 2 * self.half, one, 0)

    def add_landed(self, j, slot, chunk, first):
        def one(i, carry):
            term = self.total[j, chunk, first + i].astype(F32) + self.landed[j, slot, i].astype(F32)
            self.total[j, chunk, first + i] = term.astype(BF16)
            return carry

        lax.fori_loop(0, self.half, one, 0)

    def run(self, finish, fill=None):
        at, half = self.at, self.half
        self.combine(0)
        for j in (1, 0):
            self.copies[j][0].start()
            self.copies[j][1].start()
        self.combine(1)
        for j in (1, 0):
            self.copies[j][2].start()
        self.combine(2)
        for j in (1, 0):
            self.copies[j][3].start()
        self.combine(3)
        if fill is not None:
            fill()
        for j in (1, 0):
            self.copies[j][0].wait_recv()
            self.add_landed(j, 0, at.next_y, 0)
            self.copies[j][4].start()
            self.copies[j][1].wait_recv()
            self.add_landed(j, 1, at.last_y, half)
            self.copies[j][5].start()
        for j in (1, 0):
            for slot in (2, 3, 4, 5):
                self.copies[j][slot].wait_recv()
            if j == 0:
                self.to_ahead.wait_recv()
            for first, slots in ((0, (3, 4)), (half, (2, 5))):

                def one(i, carry, j=j, first=first, slots=slots):
                    value = self.total[j, at.y, first + i].astype(F32)
                    for slot in slots:
                        value += self.landed[j, slot, i].astype(F32)
                    if j == 1:
                        self.outgoing[first + i] = value.astype(BF16)
                    else:
                        value += self.incoming[first + i].astype(F32)
                        finish(first + i, 0.5 * value)
                    return carry

                lax.fori_loop(0, half, one, 0)
            if j == 1:
                self.to_ahead.start()

    def drain(self):
        for copy in self.across:
            copy.wait_send()
        for copies in self.copies:
            for copy in copies:
                copy.wait_send()
        self.to_ahead.wait_send()


def middle_kernel(shards, part, window, *scratch):
    at = Place(shards)
    partners = (at.partner, at.ahead, at.behind, at.right, at.left)
    signal_all(partners)
    wait_all(partners)
    count = 5 + len(REDUCE_SEMS)
    reduce = Reduce(at, part, *scratch[:count])
    reduce.start()

    def keep(i, value):
        window[0, at.y, i] = value.astype(BF16)

    reduce.run(keep)
    gather = Gather(at, window, True, *scratch[count:])
    gather.to_behind.start()
    gather.run()
    reduce.drain()


def last_kernel(shards, groups, part, p_ref, h_ref, x_ref, r_ref, q_ref, sums, *scratch):
    at = Place(shards)
    peers = [at.around(stride, size, step) for stride, size in groups for step in range(1, size)]
    partners = [at.partner, at.ahead, at.behind, at.right, at.left] + peers
    signal_all(partners)
    wait_all(partners)
    count = 5 + len(REDUCE_SEMS)
    reduce = Reduce(at, part, *scratch[:count])
    heard, g_send, g_recv = scratch[count:]
    reduce.start()
    blocks, sub, width = q_ref.shape
    zero = jnp.zeros((sub, width), F32)

    def p_of(i):
        return p_ref[pl.ds(pl.multiple_of(at.y * sub, sub), sub), pl.ds(pl.multiple_of(i * width, width), width)]

    def h_of(i):
        return h_ref[at.y, i].astype(F32)

    def fill():
        def one(i, carry):
            p, h = p_of(i), h_of(i)
            return carry[0] + p * p, carry[1] + p * h, carry[2] + h * h

        for k, value in enumerate(lax.fori_loop(0, blocks, one, (zero, zero, zero))):
            sums[k] = value

    def keep(i, value):
        q_ref[i] = value

    reduce.run(keep, fill)

    def dots(i, carry):
        q = q_ref[i]
        return carry[0] + p_of(i) * q, carry[1] + h_of(i) * q

    for k, value in enumerate(lax.fori_loop(0, blocks, dots, (zero, zero))):
        sums[3 + k] = value
    slot = 0
    sent = []
    for stride, size in groups:
        copies = []
        for step in range(1, size):
            copies.append(
                remote(sums, heard.at[slot], g_send.at[slot], g_recv.at[slot], at.around(stride, size, step))
            )
            slot += 1
        for copy in copies:
            copy.start()
        for copy in copies:
            copy.wait_recv()
        for copy in copies:
            copy.wait_send()
        for k in range(5):
            value = sums[k]
            for i in range(len(copies)):
                value += heard[slot - len(copies) + i, k]
            sums[k] = value
    pp, ph, hh, pq, hq = (
        jnp.broadcast_to(jnp.sum(sums[k], axis=1, keepdims=True), (sub, width)) for k in range(5)
    )
    first = pp / (pp + ph)
    rest = ph / (pp + ph)
    norm = rest * rest * pp - 2.0 * rest * first * ph + first * first * hh
    a = rest + norm / pp
    c = first
    curve = a * a * pp + a * (a - c) * ph - a * c * pq - c * a * ph - c * (a - c) * hh + c * c * hq
    second = norm / curve
    x_p, x_h = first + second * a, second * c
    r_p, r_h, r_q = rest - second * a, first + second * (a - c), second * c

    def out(i, carry):
        at_i = pl.ds(pl.multiple_of(i * width, width), width)
        p, h, q = p_of(i), h_of(i), q_ref[i]
        x_ref[:, at_i] = x_p * p - x_h * h
        r_ref[:, at_i] = r_p * p - r_h * h + r_q * q
        return carry

    lax.fori_loop(0, blocks, out, 0)
    reduce.drain()


def apply_kernel(first, rows, nbr_ref, u_ref, x_ref, *rest):
    if first:
        part, deg, back, along, deg_along = rest
    else:
        deg, part, h_out, back, along = rest
    step = pl.program_id(0)
    columns, width = x_ref.shape[1:]
    base = lax.axis_index("rows") * rows
    window = 3 * rows

    @pl.when(step == 0)
    def _():
        def clear(i, carry):
            back[i] = jnp.zeros((columns, width), F32)
            if first:
                deg[i] = jnp.zeros((8, width), F32)
            return carry

        lax.fori_loop(0, window, clear, 0, unroll=8)

    ones = jnp.ones((ONES, 2 * width), BF16)
    for r in range(u_ref.shape[0]):
        b = step * u_ref.shape[0] + r
        t0, t1 = nbr_ref[2 * b] - base, nbr_ref[2 * b + 1] - base
        pair = jnp.concatenate([u_ref[r, 0], u_ref[r, 1]], axis=1)
        own = x_ref[b]
        far = jnp.concatenate([x_ref[t0], x_ref[t1]], axis=1)
        if first:
            own = jnp.concatenate([own, ones[:, :width]], axis=0)
            far = jnp.concatenate([far, ones], axis=0)
        forward = lax.dot_general(far, pair, (((1,), (1,)), ((), ())), preferred_element_type=F32)
        returned = lax.dot_general(own, pair, (((1,), (0,)), ((), ())), preferred_element_type=F32)
        along[b] = forward[:columns]
        back[t0] += returned[:columns, :width]
        back[t1] += returned[:columns, width:]
        if first:
            deg_along[b] = forward[columns : columns + 8]
            deg[t0] += returned[columns : columns + 8, :width]
            deg[t1] += returned[columns : columns + 8, width:]

    @pl.when(step == pl.num_programs(0) - 1)
    def _():
        def term(i, own):
            weight = deg[i]
            minus = back[i]
            if own:
                minus += along[i]
                if first:
                    weight += deg_along[i]
                    deg[i] = weight
            x = x_ref[i].astype(F32)
            return x, jnp.concatenate([weight] * (columns // 8), axis=0) * x - minus

        for d in range(3):

            def one(i, carry, d=d):
                x, value = term(d * rows + i, d == 0)
                if first:
                    part[d * rows + i] = value.astype(BF16)
                else:
                    for g in range(RING):
                        at = slice(g * (columns // RING), (g + 1) * (columns // RING))
                        part[d, g, i] = value[at].astype(BF16)
                        if d == 0:
                            h_out[g, i] = x[at].astype(BF16)
                return carry

            lax.fori_loop(0, rows, one, 0, unroll=4)


def apply(first, nbr, upper, window, deg=None):
    rows, slots, width, _ = upper.shape
    columns = window.shape[-2]
    step_rows = min(STEP_ROWS, rows)
    whole = lambda shape: pl.BlockSpec(shape, lambda i, n: (0,) * len(shape))
    x = window.reshape(3 * rows, columns, width)
    in_specs = [pl.BlockSpec((step_rows, slots, width, width), lambda i, n: (i, 0, 0, 0)), whole(x.shape)]
    deg_shape = jax.ShapeDtypeStruct((3 * rows, 8, width), F32)
    scratch = [pltpu.VMEM(x.shape, F32), pltpu.VMEM((rows, columns, width), F32)]
    if first:
        out_shape = [jax.ShapeDtypeStruct(x.shape, BF16), deg_shape]
        scratch.append(pltpu.VMEM((rows, 8, width), F32))
        args = (nbr, upper, x)
    else:
        sub = columns // RING
        out_shape = [
            jax.ShapeDtypeStruct((3, RING, rows, sub, width), BF16),
            jax.ShapeDtypeStruct((RING, rows, sub, width), BF16),
        ]
        in_specs.append(whole(deg_shape.shape))
        args = (nbr, upper, x, deg)
    return pl.pallas_call(
        functools.partial(apply_kernel, first, rows),
        out_shape=out_shape,
        grid_spec=pltpu.PrefetchScalarGridSpec(
            num_scalar_prefetch=1,
            grid=(rows // step_rows,),
            in_specs=in_specs,
            out_specs=[whole(o.shape) for o in out_shape],
            scratch_shapes=scratch,
        ),
        compiler_params=pltpu.CompilerParams(dimension_semantics=("arbitrary",), vmem_limit_bytes=LIMIT),
        name="apply_first" if first else "apply_second",
    )(*args)


def talk(body, out_shape, scratch, collective_id, name, *args):
    return pl.pallas_call(
        body,
        out_shape=out_shape,
        in_specs=[VMEM] * len(args),
        out_specs=jax.tree.map(lambda _: VMEM, out_shape),
        scratch_shapes=scratch,
        compiler_params=pltpu.CompilerParams(
            collective_id=collective_id, has_side_effects=True, vmem_limit_bytes=LIMIT
        ),
        name=name,
    )(*args)


def per_device(pass_rates, upper_blocks, neighbours):
    rows, _, width, _ = upper_blocks.shape
    columns = pass_rates.shape[0]
    shards = lax.axis_size("rows")
    if lax.axis_size("cols") != RING or shards % 8:
        raise ValueError("mesh shape")
    quarter, sub = rows // RING, columns // RING
    groups = [(1, 2), (2, 4), (8, shards // 8)]
    messages = sum(size - 1 for _, size in groups)
    nbr = neighbours.reshape(-1)
    window_shape = jax.ShapeDtypeStruct((3, RING, quarter, columns, width), BF16)

    window = talk(
        functools.partial(halo_kernel, shards), window_shape, GATHER_SEMS, 0, "halo", pass_rates
    )
    part, deg = apply(True, nbr, upper_blocks, window)
    window = talk(
        functools.partial(middle_kernel, shards),
        window_shape,
        reduce_scratch(quarter, columns, width) + GATHER_SEMS,
        1,
        "middle",
        part.reshape(window_shape.shape),
    )
    part, h = apply(False, nbr, upper_blocks, window, deg)
    out_shape = jax.ShapeDtypeStruct((sub, rows * width), F32)
    return talk(
        functools.partial(last_kernel, shards, groups),
        (out_shape, out_shape),
        [pltpu.VMEM((rows, sub, width), F32), pltpu.VMEM((5, sub, width), F32)]
        + reduce_scratch(rows, sub, width)
        + [
            pltpu.VMEM((messages, 5, sub, width), F32),
            pltpu.SemaphoreType.DMA((messages,)),
            pltpu.SemaphoreType.DMA((messages,)),
        ],
        2,
        "last",
        part,
        pass_rates,
        h,
    )


def solution(mesh):
    in_specs = (P(None, "rows"), P("rows", "cols", None, None), P("rows", "cols"))
    out_specs = (P("cols", "rows"), P("cols", "rows"))
    return jax.shard_map(per_device, mesh=mesh, in_specs=in_specs, out_specs=out_specs, check_vma=False)
```

time: 889 us -> 175 us (0.20); the launches traced: 875 us -> 174 us
  blocking collectives: 352 us -> 0 us
  waiting for transfers between devices: 324 us -> 0 us
  Pallas kernels: 0 us -> 162 us
  other arithmetic: 97.1 us -> 0 us
  matrix products: 33.8 us -> 0 us
  starting transfers between devices: 30.3 us -> 0 us
  between operations: 14.2 us -> 0.72 us
  local copies, waits for them, and re-layouts: 22.7 us -> 10.6 us
    psum x3 -> x0, blocking collectives: 352 us -> none  [the longest x2 238 us: squares(): return lax.psum(jnp.sum(values * values, axis=1), 'rows')]
    psum x2 -> x0, waiting for transfers between devices: 173 us -> none  [per_device(): spread = lax.psum(summed, 'cols')]
    pallas_call x0 -> x5, Pallas kernels: none -> 162 us  [the longest x3 132 us: talk(): pl.pallas_call(body, out_shape=out_shape, in_specs=[VMEM] * len(args), ou...]
    ppermute x8 -> x0, waiting for transfers between devices: 152 us -> none  [from_behind(): lax.ppermute(value, axis, [(source, source + steps) for source in range(i...]
    scatter-add x2 -> x0, other arithmetic: 67.9 us -> none  [per_device(): jnp.zeros(window.shape, jnp.float32).at[:, local_index].add(transposed)]
    dot_general x4 -> x0, matrix products: 33.8 us -> none  [the longest x2 17.2 us: per_device(): jnp.einsum('bkij,cbi->cbkj', upper_blocks, own_block, preferred_element_t...]
    ppermute x8 -> x0, starting transfers between devices: 30.2 us -> none  [from_behind(): lax.ppermute(value, axis, [(source, source + steps) for source in range(i...]
    reduce_sum x3 -> x0, other arithmetic: 11.4 us -> none  [the longest x1 5.83 us: per_device(): own_weight = jnp.sum(upper_blocks, axis=(1, 3), dtype=jnp.float32)]
  transfers between devices with their start and end apart: 10 -> 0, of which waited for: 10 -> 0; matrix products, arithmetic and copies ran while one was open for 1% -> 0% of each run, Pallas kernels for 0% -> 0%
where the time goes in v1:
time: 175 us; the launch traced here: 174 us
  Pallas kernels  162 us (93%)
  local copies, waits for them, and re-layouts  10.6 us (6%)
    pallas_call x3, Pallas kernels, talk(): pl.pallas_call(body, out_shape=out_shape, in_specs=[VMEM] * len(args), ou...  132 us
    pallas_call x2, Pallas kernels, apply(): pl.pallas_call(functools.partial(apply_kernel, first, rows), out_shape=ou...  30.7 us
    unnamed x15, local copies, waits for them, and re-layouts  10.5 us

profile of v1, /device:TPU:6, one launch (start us, length us, event | category | flops | bytes accessed | tf_op | source)
XLA Modules:
  0.0 173.8 jit_solution(7175321794975383723)
XLA Ops:
  0.6 0.8 copy.5
  1.4 0.1 reshape.16.nbr_ref
  1.6 0.0 copy-start.2
  1.6 1.6 copy-done.2
  3.2 22.9 %halo.1 = bf16[3,4,32,32,128]{4,3,2,1,0:T(8,128)(2,1)S(1)} custom-call(f32[32,16384]{1,0:T(8,128)S(1)} %copy-done.2), custom_call_target="tpu_custom_call" | custom-call | tf_op jit(solution)/shard_map/halo/pallas_call | solution.py:502
  26.0 0.0 copy-start
  26.0 1.6 copy-done
  27.7 15.3 %apply_first.1 = (bf16[384,32,128]{2,1,0:T(8,128)(2,1)S(1)}, f32[384,8,128]{2,1,0:T(8,128)S(1)}) custom-call(s32[256]{0:T(256)S(1)} %reshape.16.nbr_ref, bf16[128,2,128,128]{3,2,1,0:T(8,128)(2,1)} %u_ref.3, bf16[384,32,128]{2,1,0:T(8,128)(2,1)} %bitcast.3), custom_call_target="tpu_custom_call" | custom-call | tf_op jit(solution)/shard_map/apply_first/pallas_call | solution.py:486
  43.0 0.0 copy-start.5
  43.0 1.6 copy-done.5
  44.7 50.3 %middle.1 = bf16[3,4,32,32,128]{4,3,2,1,0:T(8,128)(2,1)S(1)} custom-call(bf16[3,4,32,32,128]{4,3,2,1,0:T(8,128)(2,1)} %bitcast.5), custom_call_target="tpu_custom_call" | custom-call | tf_op jit(solution)/shard_map/middle/pallas_call | solution.py:502
  95.0 0.0 copy-start.1
  95.0 1.6 copy-done.1
  96.6 0.0 copy-start.3
  96.6 15.3 %apply_second.1 = (bf16[3,4,128,8,128]{4,3,2,1,0:T(8,128)(2,1)S(1)}, bf16[4,128,8,128]{3,2,1,0:T(8,128)(2,1)S(1)}) custom-call(s32[256]{0:T(256)S(1)} %reshape.16.nbr_ref, bf16[128,2,128,128]{3,2,1,0:T(8,128)(2,1)} %u_ref.3, bf16[384,32,128]{2,1,0:T(8,128)(2,1)} %bitcast.4, f32[384,8,128]{2,1,0:T(8,128)S(1)} %get-tuple-element.7.rest_0_), custom_call_target="tpu_custom_call" | custom-call | tf_op jit(solution)/shard_map/apply_second/pallas_call | solution.py:486
  111.9 0.0 copy-start.4
  111.9 1.6 copy-done.4
  113.6 0.0 copy-done.3
  113.6 58.6 %last.1 = (f32[8,16384]{1,0:T(8,128)S(1)}, f32[8,16384]{1,0:T(8,128)S(1)}) custom-call(bf16[3,4,128,8,128]{4,3,2,1,0:T(8,128)(2,1)} %copy-done.4, f32[32,16384]{1,0:T(8,128)S(1)} %copy-done.3, bf16[4,128,8,128]{3,2,1,0:T(8,128)(2,1)S(1)} %get-tuple-element.9.h_ref), custom_call_target="tpu_custom_call" | custom-call | tf_op jit(solution)/shard_map/last/pallas_call | solution.py:502
  172.2 0.8 copy.8
  173.0 0.8 copy.9
Async XLA Ops:
  1.6 1.6 copy-start.2
  26.0 1.6 copy-start
  43.0 1.6 copy-start.5
  95.0 1.6 copy-start.1
  96.6 17.0 %copy-start.3 = (f32[32,16384]{1,0:T(8,128)S(1)}, f32[32,16384]{1,0:T(8,128)}, u32[]{:S(2)}) copy-start(f32[32,16384]{1,0:T(8,128)} %p_ref.3) | copy-start | bytes 6291460
  111.9 1.6 copy-start.4

commit v2 on v1

--- a/solution.py
+++ b/solution.py
@@ -12,13 +12,19 @@
 BF16 = jnp.bfloat16
 RING = 4
 VMEM = pl.BlockSpec(memory_space=pltpu.VMEM)
-LIMIT = 48 * 2**20
+MIB = 2**20
 ONES = 16
-STEP_ROWS = 8
+UNROLL = 8
+TRAFFIC = {"halo": 60 * MIB, "middle": 150 * MIB, "last": 120 * MIB}
+LIMITS = {"halo": 20 * MIB, "apply": 32 * MIB, "middle": 24 * MIB, "last": 24 * MIB}
 
 
 def rem(value, count):
     return lax.rem(value, jnp.int32(count))
+
+
+def loop(count, body, carry=0):
+    return lax.fori_loop(0, count, body, carry, unroll=min(UNROLL, count))
 
 
 class Place:
@@ -132,27 +138,44 @@
         self.to_behind.wait_send()
 
 
-def halo_kernel(shards, p_ref, window, send, recv, x_send, x_recv, p_send, p_recv):
+def halo_kernel(shards, p_hbm, u_hbm, window, u_ref, p_ref, p_sem, u_sem, *sems):
     at = Place(shards)
     partners = (at.partner, at.ahead, at.behind, at.right, at.left)
     signal_all(partners)
     blocks, columns, width = window.shape[2:]
-
-    def cast(chunk):
+    order = (at.y, at.last_y, at.next_y, at.far_y)
+
+    def span(chunk):
+        return pl.ds(pl.multiple_of(chunk * (blocks * width), width), blocks * width)
+
+    loads = [
+        pltpu.make_async_copy(p_hbm.at[:, span(chunk)], p_ref.at[:, span(chunk)], p_sem.at[i])
+        for i, chunk in enumerate(order)
+    ]
+    for load in loads:
+        load.start()
+    weights = pltpu.make_async_copy(u_hbm, u_ref, u_sem)
+    weights.start()
+
+    def cast(index):
+        chunk = order[index]
+        loads[index].wait()
+
         def one(i, carry):
             first = pl.multiple_of((chunk * blocks + i) * width, width)
             window[0, chunk, i] = p_ref[:, pl.ds(first, width)].astype(BF16)
             return carry
 
-        lax.fori_loop(0, blocks, one, 0)
-
-    gather = Gather(at, window, False, send, recv, x_send, x_recv, p_send, p_recv)
-    cast(at.y)
+        loop(blocks, one)
+
+    gather = Gather(at, window, False, *sems)
+    cast(0)
     wait_all(partners)
     gather.to_behind.start()
-    for chunk in (at.last_y, at.next_y, at.far_y):
-        cast(chunk)
+    for index in (1, 2, 3):
+        cast(index)
     gather.run()
+    weights.wait()
 
 
 GATHER_SEMS = [
@@ -228,7 +251,7 @@
             self.total[kept, chunk, i] = self.part[2 * kept, chunk, i]
             return carry
 
-        lax.fori_loop(0, 2 * self.half, one, 0)
+        loop(2 * self.half, one)
 
     def add_landed(self, j, slot, chunk, first):
         def one(i, carry):
@@ -236,7 +259,7 @@
             self.total[j, chunk, first + i] = term.astype(BF16)
             return carry
 
-        lax.fori_loop(0, self.half, one, 0)
+        loop(self.half, one)
 
     def run(self, finish, fill=None):
         at, half = self.at, self.half
@@ -278,7 +301,7 @@
                         finish(first + i, 0.5 * value)
                     return carry
 
-                lax.fori_loop(0, half, one, 0)
+                loop(half, one)
             if j == 1:
                 self.to_ahead.start()
 
@@ -334,7 +357,7 @@
             p, h = p_of(i), h_of(i)
             return carry[0] + p * p, carry[1] + p * h, carry[2] + h * h
 
-        for k, value in enumerate(lax.fori_loop(0, blocks, one, (zero, zero, zero))):
+        for k, value in enumerate(loop(blocks, one, (zero, zero, zero))):
             sums[k] = value
 
     def keep(i, value):
@@ -346,15 +369,19 @@
         q = q_ref[i]
         return carry[0] + p_of(i) * q, carry[1] + h_of(i) * q
 
-    for k, value in enumerate(lax.fori_loop(0, blocks, dots, (zero, zero))):
+    for k, value in enumerate(loop(blocks, dots, (zero, zero))):
         sums[3 + k] = value
+    lanes = lax.broadcasted_iota(jnp.int32, (sub, width), 1)
+    packed = zero
+    for k in range(5):
+        packed = jnp.where(lanes == k, jnp.sum(sums[k], axis=1, keepdims=True), packed)
+    sums[0] = packed
     slot = 0
-    sent = []
     for stride, size in groups:
         copies = []
         for step in range(1, size):
             copies.append(
-                remote(sums, heard.at[slot], g_send.at[slot], g_recv.at[slot], at.around(stride, size, step))
+                remote(sums.at[0], heard.at[slot], g_send.at[slot], g_recv.at[slot], at.around(stride, size, step))
             )
             slot += 1
         for copy in copies:
@@ -363,13 +390,16 @@
             copy.wait_recv()
         for copy in copies:
             copy.wait_send()
-        for k in range(5):
-            value = sums[k]
-            for i in range(len(copies)):
-                value += heard[slot - len(copies) + i, k]
-            sums[k] = value
+        packed = sums[0]
+        for i in range(slot - len(copies), slot):
+            packed += heard[i]
+        sums[0] = packed
+    packed = sums[0]
     pp, ph, hh, pq, hq = (
-        jnp.broadcast_to(jnp.sum(sums[k], axis=1, keepdims=True), (sub, width)) for k in range(5)
+        jnp.broadcast_to(
+            jnp.sum(jnp.where(lanes == k, packed, 0.0), axis=1, keepdims=True), (sub, width)
+        )
+        for k in range(5)
     )
     first = pp / (pp + ph)
     rest = ph / (pp + ph)
@@ -388,35 +418,32 @@
         r_ref[:, at_i] = r_p * p - r_h * h + r_q * q
         return carry
 
-    lax.fori_loop(0, blocks, out, 0)
+    loop(blocks, out)
     reduce.drain()
 
 
-def apply_kernel(first, rows, nbr_ref, u_ref, x_ref, *rest):
+def apply_kernel(first, nbr_ref, u_ref, x_ref, *rest):
     if first:
         part, deg, back, along, deg_along = rest
     else:
         deg, part, h_out, back, along = rest
-    step = pl.program_id(0)
     columns, width = x_ref.shape[1:]
+    rows = u_ref.shape[0]
     base = lax.axis_index("rows") * rows
     window = 3 * rows
 
-    @pl.when(step == 0)
-    def _():
-        def clear(i, carry):
-            back[i] = jnp.zeros((columns, width), F32)
-            if first:
-                deg[i] = jnp.zeros((8, width), F32)
-            return carry
-
-        lax.fori_loop(0, window, clear, 0, unroll=8)
-
+    def clear(i, carry):
+        back[i] = jnp.zeros((columns, width), F32)
+        if first:
+            deg[i] = jnp.zeros((8, width), F32)
+        return carry
+
+    loop(window, clear)
     ones = jnp.ones((ONES, 2 * width), BF16)
-    for r in range(u_ref.shape[0]):
-        b = step * u_ref.shape[0] + r
-        t0, t1 = nbr_ref[2 * b] - base, nbr_ref[2 * b + 1] - base
-        pair = jnp.concatenate([u_ref[r, 0], u_ref[r, 1]], axis=1)
+
+    def row(b, carry):
+        t0, t1 = nbr_ref[0, b] - base, nbr_ref[1, b] - base
+        pair = jnp.concatenate([u_ref[b, 0], u_ref[b, 1]], axis=1)
         own = x_ref[b]
         far = jnp.concatenate([x_ref[t0], x_ref[t1]], axis=1)
         if first:
@@ -431,44 +458,42 @@
             deg_along[b] = forward[columns : columns + 8]
             deg[t0] += returned[columns : columns + 8, :width]
             deg[t1] += returned[columns : columns + 8, width:]
-
-    @pl.when(step == pl.num_programs(0) - 1)
-    def _():
-        def term(i, own):
-            weight = deg[i]
-            minus = back[i]
-            if own:
-                minus += along[i]
-                if first:
-                    weight += deg_along[i]
-                    deg[i] = weight
-            x = x_ref[i].astype(F32)
-            return x, jnp.concatenate([weight] * (columns // 8), axis=0) * x - minus
-
-        for d in range(3):
-
-            def one(i, carry, d=d):
-                x, value = term(d * rows + i, d == 0)
-                if first:
-                    part[d * rows + i] = value.astype(BF16)
-                else:
-                    for g in range(RING):
-                        at = slice(g * (columns // RING), (g + 1) * (columns // RING))
-                        part[d, g, i] = value[at].astype(BF16)
-                        if d == 0:
-                            h_out[g, i] = x[at].astype(BF16)
-                return carry
-
-            lax.fori_loop(0, rows, one, 0, unroll=4)
+        return carry
+
+    loop(rows, row)
+
+    def term(i, own):
+        weight = deg[i]
+        minus = back[i]
+        if own:
+            minus += along[i]
+            if first:
+                weight += deg_along[i]
+                deg[i] = weight
+        x = x_ref[i].astype(F32)
+        return x, jnp.concatenate([weight] * (columns // 8), axis=0) * x - minus
+
+    for d in range(3):
+
+        def one(i, carry, d=d):
+            x, value = term(d * rows + i, d == 0)
+            if first:
+                part[d * rows + i] = value.astype(BF16)
+            else:
+                for g in range(RING):
+                    at = slice(g * (columns // RING), (g + 1) * (columns // RING))
+                    part[d, g, i] = value[at].astype(BF16)
+                    if d == 0:
+                        h_out[g, i] = x[at].astype(BF16)
+            return carry
+
+        loop(rows, one)
 
 
 def apply(first, nbr, upper, window, deg=None):
     rows, slots, width, _ = upper.shape
     columns = window.shape[-2]
-    step_rows = min(STEP_ROWS, rows)
-    whole = lambda shape: pl.BlockSpec(shape, lambda i, n: (0,) * len(shape))
     x = window.reshape(3 * rows, columns, width)
-    in_specs = [pl.BlockSpec((step_rows, slots, width, width), lambda i, n: (i, 0, 0, 0)), whole(x.shape)]
     deg_shape = jax.ShapeDtypeStruct((3 * rows, 8, width), F32)
     scratch = [pltpu.VMEM(x.shape, F32), pltpu.VMEM((rows, columns, width), F32)]
     if first:
@@ -481,33 +506,32 @@
             jax.ShapeDtypeStruct((3, RING, rows, sub, width), BF16),
             jax.ShapeDtypeStruct((RING, rows, sub, width), BF16),
         ]
-        in_specs.append(whole(deg_shape.shape))
         args = (nbr, upper, x, deg)
     return pl.pallas_call(
-        functools.partial(apply_kernel, first, rows),
+        functools.partial(apply_kernel, first),
         out_shape=out_shape,
-        grid_spec=pltpu.PrefetchScalarGridSpec(
-            num_scalar_prefetch=1,
-            grid=(rows // step_rows,),
-            in_specs=in_specs,
-            out_specs=[whole(o.shape) for o in out_shape],
-            scratch_shapes=scratch,
+        in_specs=[pl.BlockSpec(memory_space=pltpu.SMEM)] + [VMEM] * (len(args) - 1),
+        out_specs=[VMEM] * len(out_shape),
+        scratch_shapes=scratch,
+        compiler_params=pltpu.CompilerParams(vmem_limit_bytes=LIMITS["apply"]),
+        cost_estimate=pl.CostEstimate(
+            flops=4 * rows * slots * width * width * columns, transcendentals=0, bytes_accessed=upper.size * 2
         ),
-        compiler_params=pltpu.CompilerParams(dimension_semantics=("arbitrary",), vmem_limit_bytes=LIMIT),
         name="apply_first" if first else "apply_second",
     )(*args)
 
 
-def talk(body, out_shape, scratch, collective_id, name, *args):
+def talk(body, out_shape, scratch, collective_id, name, *args, in_specs=None):
     return pl.pallas_call(
         body,
         out_shape=out_shape,
-        in_specs=[VMEM] * len(args),
+        in_specs=in_specs or [VMEM] * len(args),
         out_specs=jax.tree.map(lambda _: VMEM, out_shape),
         scratch_shapes=scratch,
         compiler_params=pltpu.CompilerParams(
-            collective_id=collective_id, has_side_effects=True, vmem_limit_bytes=LIMIT
+            collective_id=collective_id, has_side_effects=True, vmem_limit_bytes=LIMITS[name]
         ),
+        cost_estimate=pl.CostEstimate(flops=0, transcendentals=0, bytes_accessed=TRAFFIC[name]),
         name=name,
     )(*args)
 
@@ -521,13 +545,20 @@
     quarter, sub = rows // RING, columns // RING
     groups = [(1, 2), (2, 4), (8, shards // 8)]
     messages = sum(size - 1 for _, size in groups)
-    nbr = neighbours.reshape(-1)
+    nbr = neighbours.T
     window_shape = jax.ShapeDtypeStruct((3, RING, quarter, columns, width), BF16)
 
-    window = talk(
-        functools.partial(halo_kernel, shards), window_shape, GATHER_SEMS, 0, "halo", pass_rates
+    window, upper = talk(
+        functools.partial(halo_kernel, shards),
+        (window_shape, jax.ShapeDtypeStruct(upper_blocks.shape, BF16)),
+        [pltpu.VMEM(pass_rates.shape, F32), pltpu.SemaphoreType.DMA((RING,)), pltpu.SemaphoreType.DMA] + GATHER_SEMS,
+        0,
+        "halo",
+        pltpu.with_memory_space_constraint(pass_rates, pltpu.HBM),
+        pltpu.with_memory_space_constraint(upper_blocks, pltpu.HBM),
+        in_specs=[pl.BlockSpec(memory_space=pltpu.HBM)] * 2,
     )
-    part, deg = apply(True, nbr, upper_blocks, window)
+    part, deg = apply(True, nbr, upper, window)
     window = talk(
         functools.partial(middle_kernel, shards),
         window_shape,
@@ -536,7 +567,7 @@
         "middle",
         part.reshape(window_shape.shape),
     )
-    part, h = apply(False, nbr, upper_blocks, window, deg)
+    part, h = apply(False, nbr, upper, window, deg)
     out_shape = jax.ShapeDtypeStruct((sub, rows * width), F32)
     return talk(
         functools.partial(last_kernel, shards, groups),
@@ -544,7 +575,7 @@
         [pltpu.VMEM((rows, sub, width), F32), pltpu.VMEM((5, sub, width), F32)]
         + reduce_scratch(rows, sub, width)
         + [
-            pltpu.VMEM((messages, 5, sub, width), F32),
+            pltpu.VMEM((messages, sub, width), F32),
             pltpu.SemaphoreType.DMA((messages,)),
             pltpu.SemaphoreType.DMA((messages,)),
         ],

time: 175 us -> 138 us (0.79)
  Pallas kernels: 162 us -> 136 us
  local copies, waits for them, and re-layouts: 10.6 us -> 1.6 us
    pallas_call x5, Pallas kernels: 162 us -> 136 us  [the longest x3 120 us: talk(): pl.pallas_call(body, out_shape=out_shape, in_specs=in_specs or [VMEM] * l...]
    unnamed x15 -> x6, local copies, waits for them, and re-layouts: 10.5 us -> 1.6 us
where the time goes in v2:
time: 138 us
  Pallas kernels  136 us (99%)
  local copies, waits for them, and re-layouts  1.6 us (1%)
    pallas_call x3, Pallas kernels, talk(): pl.pallas_call(body, out_shape=out_shape, in_specs=in_specs or [VMEM] * l...  120 us
    pallas_call x2, Pallas kernels, apply(): pl.pallas_call(functools.partial(apply_kernel, first), out_shape=out_shap...  15.6 us

profile of v2, /device:TPU:6, one launch (start us, length us, event | category | flops | bytes accessed | tf_op | source)
XLA Modules:
  0.0 138.2 jit_solution(6361585920481916469)
XLA Ops:
  0.6 0.0 copy-start.1
  0.6 23.1 %halo.1 = (bf16[3,4,32,32,128]{4,3,2,1,0:T(8,128)(2,1)S(1)}, bf16[128,2,128,128]{3,2,1,0:T(8,128)(2,1)S(1)}) custom-call(f32[32,16384]{1,0:T(8,128)} %p_ref.1, bf16[128,2,128,128]{3,2,1,0:T(8,128)(2,1)} %u_hbm.1), custom_call_target="tpu_custom_call" | custom-call | bytes 62914560 | tf_op jit(solution)/shard_map/halo/pallas_call | solution.py:525
  23.7 0.0 copy-done.1
  23.7 7.8 %apply_first.1 = (bf16[384,32,128]{2,1,0:T(8,128)(2,1)S(1)}, f32[384,8,128]{2,1,0:T(8,128)S(1)}) custom-call(s32[2,128]{1,0:T(2,128)S(1)} %bitcast.7, bf16[128,2,128,128]{3,2,1,0:T(8,128)(2,1)S(1)} %get-tuple-element.8.u_ref, bf16[384,32,128]{2,1,0:T(8,128)(2,1)S(1)} %bitcast.6), custom_call_target="tpu_custom_call" | custom-call | flops 536870912 | bytes 8388608 | tf_op jit(solution)/shard_map/apply_first/pallas_call | solution.py:510
  31.5 48.0 %middle.1 = bf16[3,4,32,32,128]{4,3,2,1,0:T(8,128)(2,1)S(1)} custom-call(bf16[3,4,32,32,128]{4,3,2,1,0:T(8,128)(2,1)S(1)} %bitcast.5), custom_call_target="tpu_custom_call" | custom-call | bytes 157286400 | tf_op jit(solution)/shard_map/middle/pallas_call | solution.py:525
  79.5 0.0 copy-start
  79.6 7.8 %apply_second.1 = (bf16[3,4,128,8,128]{4,3,2,1,0:T(8,128)(2,1)S(1)}, bf16[4,128,8,128]{3,2,1,0:T(8,128)(2,1)S(1)}) custom-call(s32[2,128]{1,0:T(2,128)S(1)} %bitcast.8, bf16[128,2,128,128]{3,2,1,0:T(8,128)(2,1)S(1)} %get-tuple-element.8.u_ref, bf16[384,32,128]{2,1,0:T(8,128)(2,1)S(1)} %bitcast.4, f32[384,8,128]{2,1,0:T(8,128)S(1)} %get-tuple-element.11.rest_0_), custom_call_target="tpu_custom_call" | custom-call | flops 536870912 | bytes 8388608 | tf_op jit(solution)/shard_map/apply_second/pallas_call | solution.py:510
  87.4 0.0 copy-done
  87.4 49.3 %last.1 = (f32[8,16384]{1,0:T(8,128)S(1)}, f32[8,16384]{1,0:T(8,128)S(1)}) custom-call(bf16[3,4,128,8,128]{4,3,2,1,0:T(8,128)(2,1)S(1)} %get-tuple-element.12.part, f32[32,16384]{1,0:T(8,128)S(1)} %copy-done, bf16[4,128,8,128]{3,2,1,0:T(8,128)(2,1)S(1)} %get-tuple-element.13.h_ref), custom_call_target="tpu_custom_call" | custom-call | bytes 125829120 | tf_op jit(solution)/shard_map/last/pallas_call | solution.py:525
  136.6 0.8 copy.7
  137.4 0.8 copy.8
Async XLA Ops:
  0.6 23.1 %copy-start.1 = (s32[128,2]{0,1:T(2,128)S(1)}, s32[128,2]{0,1:T(2,128)}, u32[]{:S(2)}) copy-start(s32[128,2]{0,1:T(2,128)} %param.5) | copy-start | bytes 3076
  79.5 7.8 %copy-start = (f32[32,16384]{1,0:T(8,128)S(1)}, f32[32,16384]{1,0:T(8,128)}, u32[]{:S(2)}) copy-start(f32[32,16384]{1,0:T(8,128)} %p_ref.1) | copy-start | bytes 6291460

commit v3 on v2

--- a/solution.py
+++ b/solution.py
@@ -64,9 +64,9 @@
 
 
 class Spread:
-    def __init__(self, at, plane, send, recv):
-        half = plane.shape[1] // 2
-        low, high = pl.ds(0, half), pl.ds(half, half)
+    def __init__(self, at, plane, first, count, send, recv):
+        half = count // 2
+        low, high = pl.ds(first, half), pl.ds(first + half, half)
         routes = (
             (at.y, low, at.right),
             (at.y, high, at.left),
@@ -102,43 +102,70 @@
             copy.wait_send()
 
 
-class Gather:
-    def __init__(self, at, window, own, send, recv, x_send, x_recv, p_send, p_recv):
-        self.at = at
-        self.to_behind = remote(window.at[0, at.y], window.at[2, at.y], x_send, x_recv, at.behind)
-        self.planes = [Spread(at, window.at[d], send.at[i], recv.at[i]) for i, d in enumerate((0, 2)) if own or d]
-        source = 2 - 2 * at.odd
-        self.across = [
-            remote(window.at[source, chunk], window.at[1, chunk], p_send.at[i], p_recv.at[i], at.partner)
-            for i, chunk in enumerate((at.y, at.last_y, at.next_y, at.far_y))
+def gather(at, window, send, recv, low_send, low_recv, high_send, high_recv, c_send, c_recv):
+    count = window.shape[2]
+    half = count // 2
+    low, high = pl.ds(0, half), pl.ds(half, half)
+    order = (at.y, at.last_y, at.next_y, at.far_y)
+    own_high = Spread(at, window.at[0], half, half, send.at[0], recv.at[0])
+    next_low = Spread(at, window.at[2], 0, half, send.at[1], recv.at[1])
+    own_low = Spread(at, window.at[0], 0, half, send.at[2], recv.at[2])
+    x_low = remote(window.at[0, at.y, low], window.at[2, at.y, low], low_send, low_recv, at.behind)
+    x_high = [
+        remote(window.at[0, chunk, high], window.at[2, chunk, high], high_send.at[i], high_recv.at[i], at.behind)
+        for i, chunk in enumerate(order)
+    ]
+    source = 2 - 2 * at.odd
+    across = [
+        [
+            remote(
+                window.at[source, chunk, part], window.at[1, chunk, part], c_send.at[k, i], c_recv.at[k, i], at.partner
+            )
+            for i, chunk in enumerate(order)
         ]
-
-    def run(self):
-        own, ahead = (self.planes[0] if len(self.planes) > 1 else None), self.planes[-1]
-        if own is not None:
-            own.start()
-            own.relay()
-        self.to_behind.wait_recv()
-        ahead.start()
-        self.across[0].start()
-        ahead.relay()
-        if own is not None:
-            own.near()
-        ahead.near()
-        self.across[1].start()
-        self.across[2].start()
-        if own is not None:
-            own.far()
-        ahead.far()
-        self.across[3].start()
-        for plane in self.planes:
-            plane.drain()
-        for copy in self.across:
-            copy.wait()
-        self.to_behind.wait_send()
-
-
-def halo_kernel(shards, p_hbm, u_hbm, window, u_ref, p_ref, p_sem, u_sem, *sems):
+        for k, part in enumerate((low, high))
+    ]
+    x_low.start()
+    own_high.start()
+    x_high[0].start()
+    own_high.relay()
+    own_high.near()
+    x_high[1].start()
+    x_high[2].start()
+    x_low.wait_recv()
+    next_low.start()
+    across[0][0].start()
+    own_low.start()
+    own_high.far()
+    x_high[3].start()
+    next_low.relay()
+    own_low.relay()
+    x_high[0].wait_recv()
+    across[1][0].start()
+    next_low.near()
+    own_low.near()
+    across[0][1].start()
+    across[0][2].start()
+    for i in (1, 2):
+        x_high[i].wait_recv()
+        across[1][i].start()
+    next_low.far()
+    own_low.far()
+    across[0][3].start()
+    x_high[3].wait_recv()
+    across[1][3].start()
+    for spread in (own_high, next_low, own_low):
+        spread.drain()
+    x_low.wait_send()
+    for copy in x_high:
+        copy.wait_send()
+    for copy in across[0] + across[1]:
+        copy.wait()
+
+
+def halo_kernel(
+    shards, p_hbm, u_hbm, window, u_ref, p_ref, p_sem, u_sem, send, recv, q_send, q_recv, d_send, d_recv, c_send, c_recv
+):
     at = Place(shards)
     partners = (at.partner, at.ahead, at.behind, at.right, at.left)
     signal_all(partners)
@@ -168,56 +195,80 @@
 
         loop(blocks, one)
 
-    gather = Gather(at, window, False, *sems)
+    quarter = blocks // 4
+    parts = [pl.ds(k * quarter, quarter) for k in range(4)]
+    pieces = [
+        remote(window.at[0, at.y, parts[k]], window.at[2, at.y, parts[k]], q_send.at[k], q_recv.at[k], at.behind)
+        for k in range(3)
+    ]
+    direct = [
+        remote(window.at[0, chunk, parts[3]], window.at[2, chunk, parts[3]], d_send.at[i], d_recv.at[i], at.behind)
+        for i, chunk in enumerate(order)
+    ]
+    spreads = [Spread(at, window.at[2], k * quarter, quarter, send.at[k], recv.at[k]) for k in range(3)]
+    source = 2 - 2 * at.odd
+    across = [
+        remote(window.at[source, chunk], window.at[1, chunk], c_send.at[i], c_recv.at[i], at.partner)
+        for i, chunk in enumerate(order)
+    ]
     cast(0)
     wait_all(partners)
-    gather.to_behind.start()
+    for piece in pieces:
+        piece.start()
+    direct[0].start()
     for index in (1, 2, 3):
         cast(index)
-    gather.run()
+        direct[index].start()
+    for k in range(3):
+        pieces[k].wait_recv()
+        spreads[k].start()
+        if k:
+            spreads[k - 1].relay()
+    direct[0].wait_recv()
+    across[0].start()
+    spreads[2].relay()
+    for spread in spreads:
+        spread.near()
+    for i in (1, 2):
+        direct[i].wait_recv()
+        across[i].start()
+    for spread in spreads:
+        spread.far()
+    direct[3].wait_recv()
+    across[3].start()
+    for spread in spreads:
+        spread.drain()
+    for copy in pieces + direct:
+        copy.wait_send()
+    for copy in across:
+        copy.wait()
     weights.wait()
 
 
-GATHER_SEMS = [
-    pltpu.SemaphoreType.DMA((2, 6)),
-    pltpu.SemaphoreType.DMA((2, 6)),
-    pltpu.SemaphoreType.DMA,
-    pltpu.SemaphoreType.DMA,
-    pltpu.SemaphoreType.DMA((4,)),
-    pltpu.SemaphoreType.DMA((4,)),
-]
-REDUCE_SEMS = [
-    pltpu.SemaphoreType.DMA((4,)),
-    pltpu.SemaphoreType.DMA((4,)),
-    pltpu.SemaphoreType.DMA((2, 6)),
-    pltpu.SemaphoreType.DMA((2, 6)),
-    pltpu.SemaphoreType.DMA,
-    pltpu.SemaphoreType.DMA,
-]
+def pairs(*shapes):
+    return [pltpu.SemaphoreType.DMA(shape) for shape in shapes for _ in range(2)]
+
+
+HALO_SEMS = pairs((3, 6), (3,), (4,), (4,))
+GATHER_SEMS = pairs((3, 6), (), (4,), (2, 4))
+REDUCE_SEMS = pairs((4,), (3, 6), (4,), ())
 
 
 def reduce_scratch(blocks, sub, width):
     return [
         pltpu.VMEM((RING, blocks, sub, width), BF16),
         pltpu.VMEM((2, RING, blocks, sub, width), BF16),
-        pltpu.VMEM((2, 6, blocks // 2, sub, width), BF16),
-        pltpu.VMEM((blocks, sub, width), BF16),
-        pltpu.VMEM((blocks, sub, width), BF16),
+        pltpu.VMEM((3, 6, blocks // 4, sub, width), BF16),
+        pltpu.VMEM((RING, blocks // 2, sub, width), BF16),
+        pltpu.VMEM((blocks // 2, sub, width), BF16),
+        pltpu.VMEM((blocks // 2, sub, width), BF16),
     ] + REDUCE_SEMS
 
 
-class Reduce:
-    def __init__(self, at, part, crossed, total, landed, outgoing, incoming, c_send, c_recv, send, recv, x_send, x_recv):
-        self.at, self.part, self.crossed, self.total, self.landed = at, part, crossed, total, landed
-        self.outgoing, self.incoming = outgoing, incoming
-        self.half = crossed.shape[1] // 2
-        half = self.half
-        self.order = (at.far_y, at.next_y, at.last_y, at.y)
-        self.across = [
-            remote(part.at[1, chunk], crossed.at[chunk], c_send.at[i], c_recv.at[i], at.partner)
-            for i, chunk in enumerate(self.order)
-        ]
-        low, high = pl.ds(0, half), pl.ds(half, half)
+class Fold:
+    def __init__(self, at, plane, landed, first, count, send, recv):
+        self.at, self.plane, self.landed, self.first, self.half = at, plane, landed, first, count // 2
+        low, high = pl.ds(first, self.half), pl.ds(first + self.half, self.half)
         routes = (
             (at.far_y, low, at.right),
             (at.far_y, high, at.left),
@@ -227,91 +278,137 @@
             (at.last_y, high, at.left),
         )
         self.copies = [
-            [
-                remote(total.at[j, chunk, part_], landed.at[j, i], send.at[j, i], recv.at[j, i], device)
-                for i, (chunk, part_, device) in enumerate(routes)
-            ]
-            for j in range(2)
+            remote(plane.at[chunk, part], landed.at[i], send.at[i], recv.at[i], device)
+            for i, (chunk, part, device) in enumerate(routes)
         ]
-        self.to_ahead = remote(outgoing, incoming, x_send, x_recv, at.ahead)
-
-    def start(self):
-        for copy in self.across:
-            copy.start()
-
-    def combine(self, index):
-        at, chunk = self.at, self.order[index]
-        joined = 1 - at.odd
-        kept = at.odd
-        self.across[index].wait_recv()
+
+    def far(self):
+        self.copies[0].start()
+        self.copies[1].start()
+
+    def next(self):
+        self.copies[2].start()
+
+    def last(self):
+        self.copies[3].start()
+
+    def relay(self):
+        for slot, chunk, first in ((0, self.at.next_y, self.first), (1, self.at.last_y, self.first + self.half)):
+            self.copies[slot].wait_recv()
+
+            def one(i, carry, slot=slot, chunk=chunk, first=first):
+                term = self.plane[chunk, first + i].astype(F32) + self.landed[slot, i].astype(F32)
+                self.plane[chunk, first + i] = term.astype(BF16)
+                return carry
+
+            loop(self.half, one)
+            self.copies[slot + 4].start()
+
+    def result(self, take):
+        for offset, slots in ((0, (3, 4)), (self.half, (2, 5))):
+            for slot in slots:
+                self.copies[slot].wait_recv()
+
+            def one(i, carry, offset=offset, slots=slots):
+                value = self.plane[self.at.y, self.first + offset + i].astype(F32)
+                for slot in slots:
+                    value += self.landed[slot, i].astype(F32)
+                take(offset + i, value)
+                return carry
+
+            loop(self.half, one)
+
+    def drain(self):
+        for copy in self.copies:
+            copy.wait_send()
+
+
+def reduce(
+    at, finish, fill,
+    part, crossed, total, landed, behind, outgoing, incoming,
+    c_send, c_recv, send, recv, h_send, h_recv, low_send, low_recv,
+):
+    half = crossed.shape[1] // 2
+    order = (at.far_y, at.next_y, at.last_y, at.y)
+    across = [
+        remote(part.at[1, chunk], crossed.at[chunk], c_send.at[i], c_recv.at[i], at.partner)
+        for i, chunk in enumerate(order)
+    ]
+    ahead_low = Fold(at, total.at[1], landed.at[0], 0, half, send.at[0], recv.at[0])
+    own_low = Fold(at, total.at[0], landed.at[1], 0, half, send.at[1], recv.at[1])
+    own_high = Fold(at, total.at[0], landed.at[2], half, half, send.at[2], recv.at[2])
+    x_high = [
+        remote(total.at[1, chunk, pl.ds(half, half)], behind.at[chunk], h_send.at[i], h_recv.at[i], at.ahead)
+        for i, chunk in enumerate(order)
+    ]
+    x_low = remote(outgoing, incoming, low_send, low_recv, at.ahead)
+    for copy in across:
+        copy.start()
+
+    def combine(index):
+        chunk = order[index]
+        joined, kept = 1 - at.odd, at.odd
+        across[index].wait_recv()
 
         def one(i, carry):
-            term = self.part[2 * joined, chunk, i].astype(F32) + self.crossed[chunk, i].astype(F32)
-            self.total[joined, chunk, i] = term.astype(BF16)
-            self.total[kept, chunk, i] = self.part[2 * kept, chunk, i]
+            term = part[2 * joined, chunk, i].astype(F32) + crossed[chunk, i].astype(F32)
+            total[joined, chunk, i] = term.astype(BF16)
+            total[kept, chunk, i] = part[2 * kept, chunk, i]
             return carry
 
-        loop(2 * self.half, one)
-
-    def add_landed(self, j, slot, chunk, first):
+        loop(2 * half, one)
+        x_high[index].start()
+
+    def join(index):
+        chunk = order[index]
+        x_high[index].wait_recv()
+
         def one(i, carry):
-            term = self.total[j, chunk, first + i].astype(F32) + self.landed[j, slot, i].astype(F32)
-            self.total[j, chunk, first + i] = term.astype(BF16)
+            term = total[0, chunk, half + i].astype(F32) + behind[chunk, i].astype(F32)
+            total[0, chunk, half + i] = term.astype(BF16)
             return carry
 
-        loop(self.half, one)
-
-    def run(self, finish, fill=None):
-        at, half = self.at, self.half
-        self.combine(0)
-        for j in (1, 0):
-            self.copies[j][0].start()
-            self.copies[j][1].start()
-        self.combine(1)
-        for j in (1, 0):
-            self.copies[j][2].start()
-        self.combine(2)
-        for j in (1, 0):
-            self.copies[j][3].start()
-        self.combine(3)
-        if fill is not None:
-            fill()
-        for j in (1, 0):
-            self.copies[j][0].wait_recv()
-            self.add_landed(j, 0, at.next_y, 0)
-            self.copies[j][4].start()
-            self.copies[j][1].wait_recv()
-            self.add_landed(j, 1, at.last_y, half)
-            self.copies[j][5].start()
-        for j in (1, 0):
-            for slot in (2, 3, 4, 5):
-                self.copies[j][slot].wait_recv()
-            if j == 0:
-                self.to_ahead.wait_recv()
-            for first, slots in ((0, (3, 4)), (half, (2, 5))):
-
-                def one(i, carry, j=j, first=first, slots=slots):
-                    value = self.total[j, at.y, first + i].astype(F32)
-                    for slot in slots:
-                        value += self.landed[j, slot, i].astype(F32)
-                    if j == 1:
-                        self.outgoing[first + i] = value.astype(BF16)
-                    else:
-                        value += self.incoming[first + i].astype(F32)
-                        finish(first + i, 0.5 * value)
-                    return carry
-
-                loop(half, one)
-            if j == 1:
-                self.to_ahead.start()
-
-    def drain(self):
-        for copy in self.across:
+        loop(half, one)
+
+    combine(0)
+    ahead_low.far()
+    combine(1)
+    ahead_low.next()
+    combine(2)
+    ahead_low.last()
+    own_low.far()
+    own_low.next()
+    own_low.last()
+    combine(3)
+    ahead_low.relay()
+    join(0)
+    own_high.far()
+    own_low.relay()
+
+    def send_on(i, value):
+        outgoing[i] = value.astype(BF16)
+
+    ahead_low.result(send_on)
+    x_low.start()
+    join(1)
+    own_high.next()
+    join(2)
+    own_high.last()
+    if fill is not None:
+        fill()
+    join(3)
+    own_high.relay()
+    x_low.wait_recv()
+    own_low.result(lambda i, value: finish(i, 0.5 * (value + incoming[i].astype(F32))))
+    own_high.result(lambda i, value: finish(half + i, 0.5 * value))
+
+    def drain():
+        for copy in across + x_high + [x_low]:
             copy.wait_send()
-        for copies in self.copies:
-            for copy in copies:
-                copy.wait_send()
-        self.to_ahead.wait_send()
+        for fold in (ahead_low, own_low, own_high):
+            fold.drain()
+
+    return drain
 
 
 def middle_kernel(shards, part, window, *scratch):
@@ -319,18 +416,14 @@
     partners = (at.partner, at.ahead, at.behind, at.right, at.left)
     signal_all(partners)
     wait_all(partners)
-    count = 5 + len(REDUCE_SEMS)
-    reduce = Reduce(at, part, *scratch[:count])
-    reduce.start()
 
     def keep(i, value):
         window[0, at.y, i] = value.astype(BF16)
 
-    reduce.run(keep)
-    gather = Gather(at, window, True, *scratch[count:])
-    gather.to_behind.start()
-    gather.run()
-    reduce.drain()
+    count = 6 + len(REDUCE_SEMS)
+    drain = reduce(at, keep, None, part, *scratch[:count])
+    gather(at, window, *scratch[count:])
+    drain()
 
 
 def last_kernel(shards, groups, part, p_ref, h_ref, x_ref, r_ref, q_ref, sums, *scratch):
@@ -339,10 +432,8 @@
     partners = [at.partner, at.ahead, at.behind, at.right, at.left] + peers
     signal_all(partners)
     wait_all(partners)
-    count = 5 + len(REDUCE_SEMS)
-    reduce = Reduce(at, part, *scratch[:count])
+    count = 6 + len(REDUCE_SEMS)
     heard, g_send, g_recv = scratch[count:]
-    reduce.start()
     blocks, sub, width = q_ref.shape
     zero = jnp.zeros((sub, width), F32)
 
@@ -363,7 +454,7 @@
     def keep(i, value):
         q_ref[i] = value
 
-    reduce.run(keep, fill)
+    drain = reduce(at, keep, fill, part, *scratch[:count])
 
     def dots(i, carry):
         q = q_ref[i]
@@ -419,7 +510,7 @@
         return carry
 
     loop(blocks, out)
-    reduce.drain()
+    drain()
 
 
 def apply_kernel(first, nbr_ref, u_ref, x_ref, *rest):
@@ -543,7 +634,7 @@
     if lax.axis_size("cols") != RING or shards % 8:
         raise ValueError("mesh shape")
     quarter, sub = rows // RING, columns // RING
-    groups = [(1, 2), (2, 4), (8, shards // 8)]
+    groups = [(1, 8), (8, shards // 8)]
     messages = sum(size - 1 for _, size in groups)
     nbr = neighbours.T
     window_shape = jax.ShapeDtypeStruct((3, RING, quarter, columns, width), BF16)
@@ -551,7 +642,7 @@
     window, upper = talk(
         functools.partial(halo_kernel, shards),
         (window_shape, jax.ShapeDtypeStruct(upper_blocks.shape, BF16)),
-        [pltpu.VMEM(pass_rates.shape, F32), pltpu.SemaphoreType.DMA((RING,)), pltpu.SemaphoreType.DMA] + GATHER_SEMS,
+        [pltpu.VMEM(pass_rates.shape, F32), pltpu.SemaphoreType.DMA((RING,)), pltpu.SemaphoreType.DMA] + HALO_SEMS,
         0,
         "halo",
         pltpu.with_memory_space_constraint(pass_rates, pltpu.HBM),

time: 138 us -> 119 us (0.86)
  Pallas kernels: 136 us -> 116 us
    pallas_call x3, Pallas kernels: 120 us -> 101 us  [talk(): pl.pallas_call(body, out_shape=out_shape, in_specs=in_specs or [VMEM] * l...]
where the time goes in v3:
time: 119 us
  Pallas kernels  116 us (97%)
  local copies, waits for them, and re-layouts  1.6 us (1%)
    pallas_call x3, Pallas kernels, talk(): pl.pallas_call(body, out_shape=out_shape, in_specs=in_specs or [VMEM] * l...  101 us
    pallas_call x2, Pallas kernels, apply(): pl.pallas_call(functools.partial(apply_kernel, first), out_shape=out_shap...  15.6 us

profile of v3, /device:TPU:6, one launch (start us, length us, event | category | flops | bytes accessed | tf_op | source)
XLA Modules:
  0.0 118.8 jit_solution(8899799354350294381)
XLA Ops:
  0.6 0.0 copy-start.1
  0.6 20.4 %halo.1 = (bf16[3,4,32,32,128]{4,3,2,1,0:T(8,128)(2,1)S(1)}, bf16[128,2,128,128]{3,2,1,0:T(8,128)(2,1)S(1)}) custom-call(f32[32,16384]{1,0:T(8,128)} %p_ref.1, bf16[128,2,128,128]{3,2,1,0:T(8,128)(2,1)} %u_hbm.1), custom_call_target="tpu_custom_call" | custom-call | bytes 62914560 | tf_op jit(solution)/shard_map/halo/pallas_call | solution.py:616
  21.0 0.0 copy-done.1
  21.1 7.8 %apply_first.1 = (bf16[384,32,128]{2,1,0:T(8,128)(2,1)S(1)}, f32[384,8,128]{2,1,0:T(8,128)S(1)}) custom-call(s32[2,128]{1,0:T(2,128)S(1)} %bitcast.7, bf16[128,2,128,128]{3,2,1,0:T(8,128)(2,1)S(1)} %get-tuple-element.8.u_ref, bf16[384,32,128]{2,1,0:T(8,128)(2,1)S(1)} %bitcast.6), custom_call_target="tpu_custom_call" | custom-call | flops 536870912 | bytes 8388608 | tf_op jit(solution)/shard_map/apply_first/pallas_call | solution.py:601
  28.8 39.9 %middle.1 = bf16[3,4,32,32,128]{4,3,2,1,0:T(8,128)(2,1)S(1)} custom-call(bf16[3,4,32,32,128]{4,3,2,1,0:T(8,128)(2,1)S(1)} %bitcast.5), custom_call_target="tpu_custom_call" | custom-call | bytes 157286400 | tf_op jit(solution)/shard_map/middle/pallas_call | solution.py:616
  68.8 0.0 copy-start
  68.8 7.8 %apply_second.1 = (bf16[3,4,128,8,128]{4,3,2,1,0:T(8,128)(2,1)S(1)}, bf16[4,128,8,128]{3,2,1,0:T(8,128)(2,1)S(1)}) custom-call(s32[2,128]{1,0:T(2,128)S(1)} %bitcast.8, bf16[128,2,128,128]{3,2,1,0:T(8,128)(2,1)S(1)} %get-tuple-element.8.u_ref, bf16[384,32,128]{2,1,0:T(8,128)(2,1)S(1)} %bitcast.4, f32[384,8,128]{2,1,0:T(8,128)S(1)} %get-tuple-element.11.rest_0_), custom_call_target="tpu_custom_call" | custom-call | flops 536870912 | bytes 8388608 | tf_op jit(solution)/shard_map/apply_second/pallas_call | solution.py:601
  76.6 0.0 copy-done
  76.6 40.6 %last.1 = (f32[8,16384]{1,0:T(8,128)S(1)}, f32[8,16384]{1,0:T(8,128)S(1)}) custom-call(bf16[3,4,128,8,128]{4,3,2,1,0:T(8,128)(2,1)S(1)} %get-tuple-element.12.part, f32[32,16384]{1,0:T(8,128)S(1)} %copy-done, bf16[4,128,8,128]{3,2,1,0:T(8,128)(2,1)S(1)} %get-tuple-element.13.h_ref), custom_call_target="tpu_custom_call" | custom-call | bytes 125829120 | tf_op jit(solution)/shard_map/last/pallas_call | solution.py:616
  117.2 0.8 copy.7
  118.0 0.8 copy.8
Async XLA Ops:
  0.6 20.4 %copy-start.1 = (s32[128,2]{0,1:T(2,128)S(1)}, s32[128,2]{0,1:T(2,128)}, u32[]{:S(2)}) copy-start(s32[128,2]{0,1:T(2,128)} %param.5) | copy-start | bytes 3076
  68.8 7.8 %copy-start = (f32[32,16384]{1,0:T(8,128)S(1)}, f32[32,16384]{1,0:T(8,128)}, u32[]{:S(2)}) copy-start(f32[32,16384]{1,0:T(8,128)} %p_ref.1) | copy-start | bytes 6291460

commit v4 on v3

--- a/solution.py
+++ b/solution.py
@@ -24,7 +24,12 @@
 
 
 def loop(count, body, carry=0):
-    return lax.fori_loop(0, count, body, carry, unroll=min(UNROLL, count))
+    unroll = max(n for n in range(1, UNROLL + 1) if count % n == 0)
+    return lax.fori_loop(0, count, body, carry, unroll=unroll)
+
+
+def low_of(count):
+    return count * 5 // 16 * 2
 
 
 class Place:
@@ -104,12 +109,12 @@
 
 def gather(at, window, send, recv, low_send, low_recv, high_send, high_recv, c_send, c_recv):
     count = window.shape[2]
-    half = count // 2
-    low, high = pl.ds(0, half), pl.ds(half, half)
+    split = low_of(count)
+    low, high = pl.ds(0, split), pl.ds(split, count - split)
     order = (at.y, at.last_y, at.next_y, at.far_y)
-    own_high = Spread(at, window.at[0], half, half, send.at[0], recv.at[0])
-    next_low = Spread(at, window.at[2], 0, half, send.at[1], recv.at[1])
-    own_low = Spread(at, window.at[0], 0, half, send.at[2], recv.at[2])
+    own_high = Spread(at, window.at[0], split, count - split, send.at[0], recv.at[0])
+    next_low = Spread(at, window.at[2], 0, split, send.at[1], recv.at[1])
+    own_low = Spread(at, window.at[0], 0, split, send.at[2], recv.at[2])
     x_low = remote(window.at[0, at.y, low], window.at[2, at.y, low], low_send, low_recv, at.behind)
     x_high = [
         remote(window.at[0, chunk, high], window.at[2, chunk, high], high_send.at[i], high_recv.at[i], at.behind)
@@ -127,19 +132,19 @@
     ]
     x_low.start()
     own_high.start()
+    own_high.relay()
     x_high[0].start()
-    own_high.relay()
     own_high.near()
     x_high[1].start()
     x_high[2].start()
+    own_low.start()
     x_low.wait_recv()
     next_low.start()
     across[0][0].start()
-    own_low.start()
     own_high.far()
     x_high[3].start()
+    own_low.relay()
     next_low.relay()
-    own_low.relay()
     x_high[0].wait_recv()
     across[1][0].start()
     next_low.near()
@@ -182,7 +187,6 @@
     for load in loads:
         load.start()
     weights = pltpu.make_async_copy(u_hbm, u_ref, u_sem)
-    weights.start()
 
     def cast(index):
         chunk = order[index]
@@ -216,6 +220,7 @@
     for piece in pieces:
         piece.start()
     direct[0].start()
+    weights.start()
     for index in (1, 2, 3):
         cast(index)
         direct[index].start()
@@ -258,10 +263,10 @@
     return [
         pltpu.VMEM((RING, blocks, sub, width), BF16),
         pltpu.VMEM((2, RING, blocks, sub, width), BF16),
-        pltpu.VMEM((3, 6, blocks // 4, sub, width), BF16),
-        pltpu.VMEM((RING, blocks // 2, sub, width), BF16),
-        pltpu.VMEM((blocks // 2, sub, width), BF16),
-        pltpu.VMEM((blocks // 2, sub, width), BF16),
+        pltpu.VMEM((3, 6, low_of(blocks) // 2, sub, width), BF16),
+        pltpu.VMEM((RING, blocks - low_of(blocks), sub, width), BF16),
+        pltpu.VMEM((low_of(blocks), sub, width), BF16),
+        pltpu.VMEM((low_of(blocks), sub, width), BF16),
     ] + REDUCE_SEMS
 
 
@@ -278,7 +283,7 @@
             (at.last_y, high, at.left),
         )
         self.copies = [
-            remote(plane.at[chunk, part], landed.at[i], send.at[i], recv.at[i], device)
+            remote(plane.at[chunk, part], landed.at[i, pl.ds(0, self.half)], send.at[i], recv.at[i], device)
             for i, (chunk, part, device) in enumerate(routes)
         ]
 
@@ -324,21 +329,23 @@
 
 
 def reduce(
-    at, finish, fill,
+    at, finish, beside,
     part, crossed, total, landed, behind, outgoing, incoming,
     c_send, c_recv, send, recv, h_send, h_recv, low_send, low_recv,
 ):
-    half = crossed.shape[1] // 2
+    count = crossed.shape[1]
+    split = low_of(count)
+    high = count - split
     order = (at.far_y, at.next_y, at.last_y, at.y)
     across = [
         remote(part.at[1, chunk], crossed.at[chunk], c_send.at[i], c_recv.at[i], at.partner)
         for i, chunk in enumerate(order)
     ]
-    ahead_low = Fold(at, total.at[1], landed.at[0], 0, half, send.at[0], recv.at[0])
-    own_low = Fold(at, total.at[0], landed.at[1], 0, half, send.at[1], recv.at[1])
-    own_high = Fold(at, total.at[0], landed.at[2], half, half, send.at[2], recv.at[2])
+    ahead_low = Fold(at, total.at[1], landed.at[0], 0, split, send.at[0], recv.at[0])
+    own_low = Fold(at, total.at[0], landed.at[1], 0, split, send.at[1], recv.at[1])
+    own_high = Fold(at, total.at[0], landed.at[2], split, high, send.at[2], recv.at[2])
     x_high = [
-        remote(total.at[1, chunk, pl.ds(half, half)], behind.at[chunk], h_send.at[i], h_recv.at[i], at.ahead)
+        remote(total.at[1, chunk, pl.ds(split, high)], behind.at[chunk], h_send.at[i], h_recv.at[i], at.ahead)
         for i, chunk in enumerate(order)
     ]
     x_low = remote(outgoing, incoming, low_send, low_recv, at.ahead)
@@ -356,7 +363,7 @@
             total[kept, chunk, i] = part[2 * kept, chunk, i]
             return carry
 
-        loop(2 * half, one)
+        loop(count, one)
         x_high[index].start()
 
     def join(index):
@@ -364,14 +371,19 @@
         x_high[index].wait_recv()
 
         def one(i, carry):
-            term = total[0, chunk, half + i].astype(F32) + behind[chunk, i].astype(F32)
-            total[0, chunk, half + i] = term.astype(BF16)
+            term = total[0, chunk, split + i].astype(F32) + behind[chunk, i].astype(F32)
+            total[0, chunk, split + i] = term.astype(BF16)
             return carry
 
-        loop(half, one)
-
+        loop(high, one)
+
+    def send_on(i, value):
+        outgoing[i] = value.astype(BF16)
+
+    beside = beside or [lambda: None] * 5
     combine(0)
     ahead_low.far()
+    beside[0]()
     combine(1)
     ahead_low.next()
     combine(2)
@@ -380,27 +392,25 @@
     own_low.next()
     own_low.last()
     combine(3)
+    beside[1]()
     ahead_low.relay()
     join(0)
     own_high.far()
     own_low.relay()
-
-    def send_on(i, value):
-        outgoing[i] = value.astype(BF16)
-
     ahead_low.result(send_on)
     x_low.start()
+    beside[2]()
     join(1)
     own_high.next()
     join(2)
     own_high.last()
-    if fill is not None:
-        fill()
+    beside[3]()
+    own_high.relay()
     join(3)
-    own_high.relay()
+    beside[4]()
+    own_high.result(lambda i, value: finish(split + i, 0.5 * value))
     x_low.wait_recv()
     own_low.result(lambda i, value: finish(i, 0.5 * (value + incoming[i].astype(F32))))
-    own_high.result(lambda i, value: finish(half + i, 0.5 * value))
 
     def drain():
         for copy in across + x_high + [x_low]:
@@ -426,16 +436,39 @@
     drain()
 
 
-def last_kernel(shards, groups, part, p_ref, h_ref, x_ref, r_ref, q_ref, sums, *scratch):
+def last_kernel(shards, groups, part, p_ref, h_ref, hq_ref, x_ref, r_ref, sums, heard, s_send, s_recv, *scratch):
     at = Place(shards)
+    opposite = (at.s, at.far_y)
     peers = [at.around(stride, size, step) for stride, size in groups for step in range(1, size)]
-    partners = [at.partner, at.ahead, at.behind, at.right, at.left] + peers
+    partners = [at.partner, at.ahead, at.behind, at.right, at.left, opposite] + peers
     signal_all(partners)
     wait_all(partners)
-    count = 6 + len(REDUCE_SEMS)
-    heard, g_send, g_recv = scratch[count:]
-    blocks, sub, width = q_ref.shape
+    _, blocks, sub, width = h_ref.shape
     zero = jnp.zeros((sub, width), F32)
+    lanes = lax.broadcasted_iota(jnp.int32, (sub, width), 1)
+    rounds = [[(hq_ref.at[y], at_y) for y, at_y in ((at.next_y, at.right), (at.last_y, at.left), (at.far_y, opposite))]]
+    rounds += [[(sums, at.around(stride, size, step)) for step in range(1, size)] for stride, size in groups]
+    messages = []
+    for one_round in rounds:
+        first = sum(map(len, messages))
+        messages.append(
+            [
+                remote(source, heard.at[slot], s_send.at[slot], s_recv.at[slot], device)
+                for slot, (source, device) in enumerate(one_round, first)
+            ]
+        )
+
+    def tell(k):
+        for message in messages[k]:
+            message.start()
+
+    def hear(k):
+        for message in messages[k]:
+            message.wait_recv()
+        for message in messages[k]:
+            message.wait_send()
+        first = sum(map(len, messages[:k]))
+        return sum((heard[slot] for slot in range(first, first + len(messages[k]))), zero)
 
     def p_of(i):
         return p_ref[pl.ds(pl.multiple_of(at.y * sub, sub), sub), pl.ds(pl.multiple_of(i * width, width), width)]
@@ -443,73 +476,55 @@
     def h_of(i):
         return h_ref[at.y, i].astype(F32)
 
-    def fill():
+    def square():
         def one(i, carry):
             p, h = p_of(i), h_of(i)
             return carry[0] + p * p, carry[1] + p * h, carry[2] + h * h
 
+        packed = zero
         for k, value in enumerate(loop(blocks, one, (zero, zero, zero))):
-            sums[k] = value
-
-    def keep(i, value):
-        q_ref[i] = value
-
-    drain = reduce(at, keep, fill, part, *scratch[:count])
-
-    def dots(i, carry):
-        q = q_ref[i]
-        return carry[0] + p_of(i) * q, carry[1] + h_of(i) * q
-
-    for k, value in enumerate(loop(blocks, dots, (zero, zero))):
-        sums[3 + k] = value
-    lanes = lax.broadcasted_iota(jnp.int32, (sub, width), 1)
-    packed = zero
-    for k in range(5):
-        packed = jnp.where(lanes == k, jnp.sum(sums[k], axis=1, keepdims=True), packed)
-    sums[0] = packed
-    slot = 0
-    for stride, size in groups:
-        copies = []
-        for step in range(1, size):
-            copies.append(
-                remote(sums.at[0], heard.at[slot], g_send.at[slot], g_recv.at[slot], at.around(stride, size, step))
-            )
-            slot += 1
-        for copy in copies:
-            copy.start()
-        for copy in copies:
-            copy.wait_recv()
-        for copy in copies:
-            copy.wait_send()
-        packed = sums[0]
-        for i in range(slot - len(copies), slot):
-            packed += heard[i]
-        sums[0] = packed
-    packed = sums[0]
-    pp, ph, hh, pq, hq = (
-        jnp.broadcast_to(
-            jnp.sum(jnp.where(lanes == k, packed, 0.0), axis=1, keepdims=True), (sub, width)
+            packed = jnp.where(lanes == k, jnp.sum(value, axis=1, keepdims=True), packed)
+        sums[...] = packed
+
+    def start_sums():
+        value = jnp.sum(hear(0) + hq_ref[at.y], axis=1, keepdims=True)
+        sums[...] = jnp.where(lanes == 3, value, sums[...])
+        tell(1)
+
+    def pass_sums():
+        sums[...] = sums[...] + hear(1)
+        tell(2)
+
+    scale = []
+
+    def end_sums():
+        packed = sums[...] + hear(2)
+        pp, ph, hh, hq = (
+            jnp.broadcast_to(jnp.sum(jnp.where(lanes == k, packed, 0.0), axis=1, keepdims=True), (sub, width))
+            for k in range(4)
         )
-        for k in range(5)
-    )
-    first = pp / (pp + ph)
-    rest = ph / (pp + ph)
-    norm = rest * rest * pp - 2.0 * rest * first * ph + first * first * hh
-    a = rest + norm / pp
-    c = first
-    curve = a * a * pp + a * (a - c) * ph - a * c * pq - c * a * ph - c * (a - c) * hh + c * c * hq
-    second = norm / curve
-    x_p, x_h = first + second * a, second * c
-    r_p, r_h, r_q = rest - second * a, first + second * (a - c), second * c
-
-    def out(i, carry):
-        at_i = pl.ds(pl.multiple_of(i * width, width), width)
-        p, h, q = p_of(i), h_of(i), q_ref[i]
-        x_ref[:, at_i] = x_p * p - x_h * h
-        r_ref[:, at_i] = r_p * p - r_h * h + r_q * q
-        return carry
-
-    loop(blocks, out)
+        first = pp / (pp + ph)
+        rest = ph / (pp + ph)
+        norm = rest * rest * pp - 2.0 * rest * first * ph + first * first * hh
+        a = rest + norm / pp
+        c = first
+        curve = a * a * pp + a * (a - 2.0 * c) * ph + c * (c - 2.0 * a) * hh + c * c * hq
+        second = norm / curve
+        x_p, x_h = first + second * a, second * c
+        scale.extend((rest - second * a, first + second * (a - c), second * c))
+
+        def one(i, carry):
+            x_ref[:, pl.ds(pl.multiple_of(i * width, width), width)] = x_p * p_of(i) - x_h * h_of(i)
+            return carry
+
+        loop(blocks, one)
+
+    def keep(i, q):
+        r_p, r_h, r_q = scale
+        r_ref[:, pl.ds(pl.multiple_of(i * width, width), width)] = r_p * p_of(i) - r_h * h_of(i) + r_q * q
+
+    tell(0)
+    drain = reduce(at, keep, [square, start_sums, pass_sums, lambda: None, end_sums], part, *scratch)
     drain()
 
 
@@ -517,7 +532,7 @@
     if first:
         part, deg, back, along, deg_along = rest
     else:
-        deg, part, h_out, back, along = rest
+        deg, part, h_out, hq_out, back, along = rest
     columns, width = x_ref.shape[1:]
     rows = u_ref.shape[0]
     base = lax.axis_index("rows") * rows
@@ -564,10 +579,12 @@
         x = x_ref[i].astype(F32)
         return x, jnp.concatenate([weight] * (columns // 8), axis=0) * x - minus
 
+    dots = jnp.zeros((columns, width), F32)
     for d in range(3):
 
         def one(i, carry, d=d):
             x, value = term(d * rows + i, d == 0)
+            carry += x * value
             if first:
                 part[d * rows + i] = value.astype(BF16)
             else:
@@ -578,7 +595,10 @@
                         h_out[g, i] = x[at].astype(BF16)
             return carry
 
-        loop(rows, one)
+        dots = loop(rows, one, dots)
+    if not first:
+        for g in range(RING):
+            hq_out[g] = 0.5 * dots[g * (columns // RING) : (g + 1) * (columns // RING)]
 
 
 def apply(first, nbr, upper, window, deg=None):
@@ -596,6 +616,7 @@
         out_shape = [
             jax.ShapeDtypeStruct((3, RING, rows, sub, width), BF16),
             jax.ShapeDtypeStruct((RING, rows, sub, width), BF16),
+            jax.ShapeDtypeStruct((RING, sub, width), F32),
         ]
         args = (nbr, upper, x, deg)
     return pl.pallas_call(
@@ -635,7 +656,7 @@
         raise ValueError("mesh shape")
     quarter, sub = rows // RING, columns // RING
     groups = [(1, 8), (8, shards // 8)]
-    messages = sum(size - 1 for _, size in groups)
+    messages = RING - 1 + sum(size - 1 for _, size in groups)
     nbr = neighbours.T
     window_shape = jax.ShapeDtypeStruct((3, RING, quarter, columns, width), BF16)
 
@@ -658,23 +679,20 @@
         "middle",
         part.reshape(window_shape.shape),
     )
-    part, h = apply(False, nbr, upper, window, deg)
+    part, h, hq = apply(False, nbr, upper, window, deg)
     out_shape = jax.ShapeDtypeStruct((sub, rows * width), F32)
     return talk(
         functools.partial(last_kernel, shards, groups),
         (out_shape, out_shape),
-        [pltpu.VMEM((rows, sub, width), F32), pltpu.VMEM((5, sub, width), F32)]
-        + reduce_scratch(rows, sub, width)
-        + [
-            pltpu.VMEM((messages, sub, width), F32),
-            pltpu.SemaphoreType.DMA((messages,)),
-            pltpu.SemaphoreType.DMA((messages,)),
-        ],
+        [pltpu.VMEM((sub, width), F32), pltpu.VMEM((messages, sub, width), F32)]
+        + pairs((messages,))
+        + reduce_scratch(rows, sub, width),
         2,
         "last",
         part,
         pass_rates,
         h,
+        hq,
     )
 
 

time: 119 us -> 111 us (0.933); the launches traced: 119 us -> 109 us
  Pallas kernels: 116 us -> 107 us
    pallas_call x3, Pallas kernels: 101 us -> 90.8 us  [talk(): pl.pallas_call(body, out_shape=out_shape, in_specs=in_specs or [VMEM] * l...]
where the time goes in v4:
time: 111 us; the launch traced here: 109 us
  Pallas kernels  107 us (96%)
  local copies, waits for them, and re-layouts  1.6 us (1%)
    pallas_call x3, Pallas kernels, talk(): pl.pallas_call(body, out_shape=out_shape, in_specs=in_specs or [VMEM] * l...  90.8 us
    pallas_call x2, Pallas kernels, apply(): pl.pallas_call(functools.partial(apply_kernel, first), out_shape=out_shap...  16 us

profile of v4, /device:TPU:6, one launch (start us, length us, event | category | flops | bytes accessed | tf_op | source)
XLA Modules:
  0.0 109.1 jit_solution(15863068148794891490)
XLA Ops:
  0.6 0.0 copy-start.1
  0.6 20.4 %halo.1 = (bf16[3,4,32,32,128]{4,3,2,1,0:T(8,128)(2,1)S(1)}, bf16[128,2,128,128]{3,2,1,0:T(8,128)(2,1)S(1)}) custom-call(f32[32,16384]{1,0:T(8,128)} %p_ref.1, bf16[128,2,128,128]{3,2,1,0:T(8,128)(2,1)} %u_hbm.1), custom_call_target="tpu_custom_call" | custom-call | bytes 62914560 | tf_op jit(solution)/shard_map/halo/pallas_call | solution.py:637
  21.0 0.0 copy-done.1
  21.1 7.8 %apply_first.1 = (bf16[384,32,128]{2,1,0:T(8,128)(2,1)S(1)}, f32[384,8,128]{2,1,0:T(8,128)S(1)}) custom-call(s32[2,128]{1,0:T(2,128)S(1)} %bitcast.7, bf16[128,2,128,128]{3,2,1,0:T(8,128)(2,1)S(1)} %get-tuple-element.9.u_ref, bf16[384,32,128]{2,1,0:T(8,128)(2,1)S(1)} %bitcast.6), custom_call_target="tpu_custom_call" | custom-call | flops 536870912 | bytes 8388608 | tf_op jit(solution)/shard_map/apply_first/pallas_call | solution.py:622
  28.8 38.4 %middle.1 = bf16[3,4,32,32,128]{4,3,2,1,0:T(8,128)(2,1)S(1)} custom-call(bf16[3,4,32,32,128]{4,3,2,1,0:T(8,128)(2,1)S(1)} %bitcast.5), custom_call_target="tpu_custom_call" | custom-call | bytes 157286400 | tf_op jit(solution)/shard_map/middle/pallas_call | solution.py:637
  67.2 0.0 copy-start
  67.2 8.2 %apply_second.1 = (bf16[3,4,128,8,128]{4,3,2,1,0:T(8,128)(2,1)S(1)}, bf16[4,128,8,128]{3,2,1,0:T(8,128)(2,1)S(1)}, f32[4,8,128]{2,1,0:T(8,128)S(1)}) custom-call(s32[2,128]{1,0:T(2,128)S(1)} %bitcast.8, bf16[128,2,128,128]{3,2,1,0:T(8,128)(2,1)S(1)} %get-tuple-element.9.u_ref, bf16[384,32,128]{2,1,0:T(8,128)(2,1)S(1)} %bitcast.4, ...), custom_call_target="tpu_custom_call" | custom-call | flops 536870912 | bytes 8388608 | tf_op jit(solution)/shard_map/apply_second/pallas_call | solution.py:622
  75.4 0.0 copy-done
  75.4 32.1 %last.1 = (f32[8,16384]{1,0:T(8,128)S(1)}, f32[8,16384]{1,0:T(8,128)S(1)}) custom-call(bf16[3,4,128,8,128]{4,3,2,1,0:T(8,128)(2,1)S(1)} %get-tuple-element.13.part, f32[32,16384]{1,0:T(8,128)S(1)} %copy-done, bf16[4,128,8,128]{3,2,1,0:T(8,128)(2,1)S(1)} %get-tuple-element.14.h_ref, f32[4,8,128]{2,1,0:T(8,128)S(1)} %get-tuple-element.15.hq_ref), custom_call_target="tpu_custom_call" | custom-call | bytes 125829120 | tf_op jit(solution)/shard_map/last/pallas_call | solution.py:637
  107.5 0.8 copy.7
  108.3 0.8 copy.8
Async XLA Ops:
  0.6 20.4 %copy-start.1 = (s32[128,2]{0,1:T(2,128)S(1)}, s32[128,2]{0,1:T(2,128)}, u32[]{:S(2)}) copy-start(s32[128,2]{0,1:T(2,128)} %param.5) | copy-start | bytes 3076
  67.2 8.2 %copy-start = (f32[32,16384]{1,0:T(8,128)S(1)}, f32[32,16384]{1,0:T(8,128)}, u32[]{:S(2)}) copy-start(f32[32,16384]{1,0:T(8,128)} %p_ref.1) | copy-start | bytes 6291460

commit v5 on v4

--- a/solution.py
+++ b/solution.py
@@ -15,6 +15,7 @@
 MIB = 2**20
 ONES = 16
 UNROLL = 8
+ROW_UNROLL = 32
 TRAFFIC = {"halo": 60 * MIB, "middle": 150 * MIB, "last": 120 * MIB}
 LIMITS = {"halo": 20 * MIB, "apply": 32 * MIB, "middle": 24 * MIB, "last": 24 * MIB}
 
@@ -26,6 +27,10 @@
 def loop(count, body, carry=0):
     unroll = max(n for n in range(1, UNROLL + 1) if count % n == 0)
     return lax.fori_loop(0, count, body, carry, unroll=unroll)
+
+
+def nothing():
+    pass
 
 
 def low_of(count):
@@ -130,10 +135,11 @@
         ]
         for k, part in enumerate((low, high))
     ]
+    own_high.start()
+    x_high[0].start()
+    yield
     x_low.start()
-    own_high.start()
     own_high.relay()
-    x_high[0].start()
     own_high.near()
     x_high[1].start()
     x_high[2].start()
@@ -166,6 +172,7 @@
         copy.wait_send()
     for copy in across[0] + across[1]:
         copy.wait()
+    yield
 
 
 def halo_kernel(
@@ -199,17 +206,18 @@
 
         loop(blocks, one)
 
-    quarter = blocks // 4
-    parts = [pl.ds(k * quarter, quarter) for k in range(4)]
+    split = low_of(blocks)
+    piece = split // 2
+    parts = [pl.ds(0, piece), pl.ds(piece, piece), pl.ds(split, blocks - split)]
     pieces = [
         remote(window.at[0, at.y, parts[k]], window.at[2, at.y, parts[k]], q_send.at[k], q_recv.at[k], at.behind)
-        for k in range(3)
+        for k in range(2)
     ]
     direct = [
-        remote(window.at[0, chunk, parts[3]], window.at[2, chunk, parts[3]], d_send.at[i], d_recv.at[i], at.behind)
+        remote(window.at[0, chunk, parts[2]], window.at[2, chunk, parts[2]], d_send.at[i], d_recv.at[i], at.behind)
         for i, chunk in enumerate(order)
     ]
-    spreads = [Spread(at, window.at[2], k * quarter, quarter, send.at[k], recv.at[k]) for k in range(3)]
+    spreads = [Spread(at, window.at[2], k * piece, piece, send.at[k], recv.at[k]) for k in range(2)]
     source = 2 - 2 * at.odd
     across = [
         remote(window.at[source, chunk], window.at[1, chunk], c_send.at[i], c_recv.at[i], at.partner)
@@ -217,21 +225,21 @@
     ]
     cast(0)
     wait_all(partners)
-    for piece in pieces:
-        piece.start()
-    direct[0].start()
+    pieces[0].start()
+    pieces[1].start()
     weights.start()
     for index in (1, 2, 3):
         cast(index)
-        direct[index].start()
-    for k in range(3):
-        pieces[k].wait_recv()
-        spreads[k].start()
-        if k:
-            spreads[k - 1].relay()
+    pieces[0].wait_recv()
+    spreads[0].start()
+    for copy in direct:
+        copy.start()
+    pieces[1].wait_recv()
+    spreads[1].start()
+    spreads[0].relay()
     direct[0].wait_recv()
     across[0].start()
-    spreads[2].relay()
+    spreads[1].relay()
     for spread in spreads:
         spread.near()
     for i in (1, 2):
@@ -254,7 +262,7 @@
     return [pltpu.SemaphoreType.DMA(shape) for shape in shapes for _ in range(2)]
 
 
-HALO_SEMS = pairs((3, 6), (3,), (4,), (4,))
+HALO_SEMS = pairs((2, 6), (2,), (4,), (4,))
 GATHER_SEMS = pairs((3, 6), (), (4,), (2, 4))
 REDUCE_SEMS = pairs((4,), (3, 6), (4,), ())
 
@@ -380,7 +388,6 @@
     def send_on(i, value):
         outgoing[i] = value.astype(BF16)
 
-    beside = beside or [lambda: None] * 5
     combine(0)
     ahead_low.far()
     beside[0]()
@@ -409,6 +416,7 @@
     join(3)
     beside[4]()
     own_high.result(lambda i, value: finish(split + i, 0.5 * value))
+    beside[5]()
     x_low.wait_recv()
     own_low.result(lambda i, value: finish(i, 0.5 * (value + incoming[i].astype(F32))))
 
@@ -431,8 +439,9 @@
         window[0, at.y, i] = value.astype(BF16)
 
     count = 6 + len(REDUCE_SEMS)
-    drain = reduce(at, keep, None, part, *scratch[:count])
-    gather(at, window, *scratch[count:])
+    steps = gather(at, window, *scratch[count:])
+    drain = reduce(at, keep, [nothing] * 5 + [lambda: next(steps)], part, *scratch[:count])
+    next(steps)
     drain()
 
 
@@ -524,7 +533,7 @@
         r_ref[:, pl.ds(pl.multiple_of(i * width, width), width)] = r_p * p_of(i) - r_h * h_of(i) + r_q * q
 
     tell(0)
-    drain = reduce(at, keep, [square, start_sums, pass_sums, lambda: None, end_sums], part, *scratch)
+    drain = reduce(at, keep, [square, start_sums, pass_sums, nothing, end_sums, nothing], part, *scratch)
     drain()
 
 
@@ -566,7 +575,7 @@
             deg[t1] += returned[columns : columns + 8, width:]
         return carry
 
-    loop(rows, row)
+    lax.fori_loop(0, rows, row, 0, unroll=min(ROW_UNROLL, rows))
 
     def term(i, own):
         weight = deg[i]

time: 111 us -> 107 us (0.964); the launches traced: 109 us -> 107 us
  Pallas kernels: 107 us -> 105 us
    pallas_call x2, Pallas kernels: 16 us -> 13 us  [apply(): pl.pallas_call(functools.partial(apply_kernel, first), out_shape=out_shap...]
where the time goes in v5:
time: 107 us
  Pallas kernels  105 us (98%)
  local copies, waits for them, and re-layouts  1.6 us (1%)
    pallas_call x3, Pallas kernels, talk(): pl.pallas_call(body, out_shape=out_shape, in_specs=in_specs or [VMEM] * l...  91.5 us
    pallas_call x2, Pallas kernels, apply(): pl.pallas_call(functools.partial(apply_kernel, first), out_shape=out_shap...  13 us

profile of v5, /device:TPU:6, one launch (start us, length us, event | category | flops | bytes accessed | tf_op | source)
XLA Modules:
  0.0 106.8 jit_solution(17232925082251466077)
XLA Ops:
  0.6 0.0 copy-start.1
  0.6 19.0 %halo.1 = (bf16[3,4,32,32,128]{4,3,2,1,0:T(8,128)(2,1)S(1)}, bf16[128,2,128,128]{3,2,1,0:T(8,128)(2,1)S(1)}) custom-call(f32[32,16384]{1,0:T(8,128)} %p_ref.1, bf16[128,2,128,128]{3,2,1,0:T(8,128)(2,1)} %u_hbm.1), custom_call_target="tpu_custom_call" | custom-call | bytes 62914560 | tf_op jit(solution)/shard_map/halo/pallas_call | solution.py:646
  19.6 0.0 copy-done.1
  19.6 6.3 %apply_first.1 = (bf16[384,32,128]{2,1,0:T(8,128)(2,1)S(1)}, f32[384,8,128]{2,1,0:T(8,128)S(1)}) custom-call(s32[2,128]{1,0:T(2,128)S(1)} %bitcast.7, bf16[128,2,128,128]{3,2,1,0:T(8,128)(2,1)S(1)} %get-tuple-element.9.u_ref, bf16[384,32,128]{2,1,0:T(8,128)(2,1)S(1)} %bitcast.6), custom_call_target="tpu_custom_call" | custom-call | flops 536870912 | bytes 8388608 | tf_op jit(solution)/shard_map/apply_first/pallas_call | solution.py:631
  25.9 40.0 %middle.1 = bf16[3,4,32,32,128]{4,3,2,1,0:T(8,128)(2,1)S(1)} custom-call(bf16[3,4,32,32,128]{4,3,2,1,0:T(8,128)(2,1)S(1)} %bitcast.5), custom_call_target="tpu_custom_call" | custom-call | bytes 157286400 | tf_op jit(solution)/shard_map/middle/pallas_call | solution.py:646
  65.9 0.0 copy-start
  65.9 6.7 %apply_second.1 = (bf16[3,4,128,8,128]{4,3,2,1,0:T(8,128)(2,1)S(1)}, bf16[4,128,8,128]{3,2,1,0:T(8,128)(2,1)S(1)}, f32[4,8,128]{2,1,0:T(8,128)S(1)}) custom-call(s32[2,128]{1,0:T(2,128)S(1)} %bitcast.8, bf16[128,2,128,128]{3,2,1,0:T(8,128)(2,1)S(1)} %get-tuple-element.9.u_ref, bf16[384,32,128]{2,1,0:T(8,128)(2,1)S(1)} %bitcast.4, ...), custom_call_target="tpu_custom_call" | custom-call | flops 536870912 | bytes 8388608 | tf_op jit(solution)/shard_map/apply_second/pallas_call | solution.py:631
  72.7 0.0 copy-done
  72.7 32.6 %last.1 = (f32[8,16384]{1,0:T(8,128)S(1)}, f32[8,16384]{1,0:T(8,128)S(1)}) custom-call(bf16[3,4,128,8,128]{4,3,2,1,0:T(8,128)(2,1)S(1)} %get-tuple-element.13.part, f32[32,16384]{1,0:T(8,128)S(1)} %copy-done, bf16[4,128,8,128]{3,2,1,0:T(8,128)(2,1)S(1)} %get-tuple-element.14.h_ref, f32[4,8,128]{2,1,0:T(8,128)S(1)} %get-tuple-element.15.hq_ref), custom_call_target="tpu_custom_call" | custom-call | bytes 125829120 | tf_op jit(solution)/shard_map/last/pallas_call | solution.py:646
  105.2 0.8 copy.7
  106.0 0.8 copy.8
Async XLA Ops:
  0.6 19.0 %copy-start.1 = (s32[128,2]{0,1:T(2,128)S(1)}, s32[128,2]{0,1:T(2,128)}, u32[]{:S(2)}) copy-start(s32[128,2]{0,1:T(2,128)} %param.5) | copy-start | bytes 3076
  65.9 6.7 %copy-start = (f32[32,16384]{1,0:T(8,128)S(1)}, f32[32,16384]{1,0:T(8,128)}, u32[]{:S(2)}) copy-start(f32[32,16384]{1,0:T(8,128)} %p_ref.1) | copy-start | bytes 6291460

commit v6 on v5

--- a/solution.py
+++ b/solution.py
@@ -279,7 +279,7 @@
 
 
 class Fold:
-    def __init__(self, at, plane, landed, first, count, send, recv):
+    def __init__(self, at, plane, whole, landed, first, count, send, recv):
         self.at, self.plane, self.landed, self.first, self.half = at, plane, landed, first, count // 2
         low, high = pl.ds(first, self.half), pl.ds(first + self.half, self.half)
         routes = (
@@ -290,10 +290,13 @@
             (at.next_y, low, at.right),
             (at.last_y, high, at.left),
         )
-        self.copies = [
-            remote(plane.at[chunk, part], landed.at[i, pl.ds(0, self.half)], send.at[i], recv.at[i], device)
-            for i, (chunk, part, device) in enumerate(routes)
-        ]
+        self.copies, self.soon = (
+            [
+                remote(source.at[chunk, part], landed.at[i, pl.ds(0, self.half)], send.at[i], recv.at[i], device)
+                for i, (chunk, part, device) in enumerate(routes[:most])
+            ]
+            for source, most in ((plane, 6), (whole, 4 if whole is not None else 0))
+        )
 
     def far(self):
         self.copies[0].start()
@@ -304,6 +307,10 @@
 
     def last(self):
         self.copies[3].start()
+
+    def begin(self):
+        for copy in self.soon:
+            copy.start()
 
     def relay(self):
         for slot, chunk, first in ((0, self.at.next_y, self.first), (1, self.at.last_y, self.first + self.half)):
@@ -349,16 +356,31 @@
         remote(part.at[1, chunk], crossed.at[chunk], c_send.at[i], c_recv.at[i], at.partner)
         for i, chunk in enumerate(order)
     ]
-    ahead_low = Fold(at, total.at[1], landed.at[0], 0, split, send.at[0], recv.at[0])
-    own_low = Fold(at, total.at[0], landed.at[1], 0, split, send.at[1], recv.at[1])
-    own_high = Fold(at, total.at[0], landed.at[2], split, high, send.at[2], recv.at[2])
-    x_high = [
-        remote(total.at[1, chunk, pl.ds(split, high)], behind.at[chunk], h_send.at[i], h_recv.at[i], at.ahead)
-        for i, chunk in enumerate(order)
-    ]
+    ahead_low = Fold(at, total.at[1], part.at[2], landed.at[0], 0, split, send.at[0], recv.at[0])
+    own_low = Fold(at, total.at[0], part.at[0], landed.at[1], 0, split, send.at[1], recv.at[1])
+    own_high = Fold(at, total.at[0], None, landed.at[2], split, high, send.at[2], recv.at[2])
+    x_high, x_soon = (
+        [
+            remote(source.at[chunk, pl.ds(split, high)], behind.at[chunk], h_send.at[i], h_recv.at[i], at.ahead)
+            for i, chunk in enumerate(order)
+        ]
+        for source in (total.at[1], part.at[2])
+    )
     x_low = remote(outgoing, incoming, low_send, low_recv, at.ahead)
     for copy in across:
         copy.start()
+
+    @pl.when(at.odd == 1)
+    def _():
+        for copy in x_soon[:1]:
+            copy.start()
+        ahead_low.begin()
+        for copy in x_soon[1:]:
+            copy.start()
+
+    @pl.when(at.odd == 0)
+    def _():
+        own_low.begin()
 
     def combine(index):
         chunk = order[index]
@@ -372,7 +394,6 @@
             return carry
 
         loop(count, one)
-        x_high[index].start()
 
     def join(index):
         chunk = order[index]
@@ -388,22 +409,27 @@
     def send_on(i, value):
         outgoing[i] = value.astype(BF16)
 
-    combine(0)
-    ahead_low.far()
-    beside[0]()
-    combine(1)
-    ahead_low.next()
-    combine(2)
-    ahead_low.last()
-    own_low.far()
-    own_low.next()
-    own_low.last()
-    combine(3)
+    for index in range(4):
+        combine(index)
+
+        @pl.when(at.odd == 0)
+        def _(index=index):
+            x_high[index].start()
+            if index < 3:
+                (ahead_low.far, ahead_low.next, ahead_low.last)[index]()
+
+        @pl.when(at.odd == 1)
+        def _(index=index):
+            if index < 3:
+                (own_low.far, own_low.next, own_low.last)[index]()
+
+        if index == 0:
+            beside[0]()
     beside[1]()
     ahead_low.relay()
+    own_low.relay()
     join(0)
     own_high.far()
-    own_low.relay()
     ahead_low.result(send_on)
     x_low.start()
     beside[2]()

time: 107 us -> 105 us (0.981)
  Pallas kernels: 105 us -> 103 us
    pallas_call x3, Pallas kernels: 91.5 us -> 89.7 us  [talk(): pl.pallas_call(body, out_shape=out_shape, in_specs=in_specs or [VMEM] * l...]
where the time goes in v6:
time: 105 us
  Pallas kernels  103 us (98%)
  local copies, waits for them, and re-layouts  1.6 us (2%)
    pallas_call x3, Pallas kernels, talk(): pl.pallas_call(body, out_shape=out_shape, in_specs=in_specs or [VMEM] * l...  89.7 us
    pallas_call x2, Pallas kernels, apply(): pl.pallas_call(functools.partial(apply_kernel, first), out_shape=out_shap...  13 us

profile of v6, /device:TPU:6, one launch (start us, length us, event | category | flops | bytes accessed | tf_op | source)
XLA Modules:
  0.0 105.0 jit_solution(3456667949168575760)
XLA Ops:
  0.6 0.0 copy-start.1
  0.6 19.0 %halo.1 = (bf16[3,4,32,32,128]{4,3,2,1,0:T(8,128)(2,1)S(1)}, bf16[128,2,128,128]{3,2,1,0:T(8,128)(2,1)S(1)}) custom-call(f32[32,16384]{1,0:T(8,128)} %p_ref.1, bf16[128,2,128,128]{3,2,1,0:T(8,128)(2,1)} %u_hbm.1), custom_call_target="tpu_custom_call" | custom-call | bytes 62914560 | tf_op jit(solution)/shard_map/halo/pallas_call | solution.py:672
  19.6 0.0 copy-done.1
  19.6 6.3 %apply_first.1 = (bf16[384,32,128]{2,1,0:T(8,128)(2,1)S(1)}, f32[384,8,128]{2,1,0:T(8,128)S(1)}) custom-call(s32[2,128]{1,0:T(2,128)S(1)} %bitcast.7, bf16[128,2,128,128]{3,2,1,0:T(8,128)(2,1)S(1)} %get-tuple-element.9.u_ref, bf16[384,32,128]{2,1,0:T(8,128)(2,1)S(1)} %bitcast.6), custom_call_target="tpu_custom_call" | custom-call | flops 536870912 | bytes 8388608 | tf_op jit(solution)/shard_map/apply_first/pallas_call | solution.py:657
  25.9 39.9 %middle.1 = bf16[3,4,32,32,128]{4,3,2,1,0:T(8,128)(2,1)S(1)} custom-call(bf16[3,4,32,32,128]{4,3,2,1,0:T(8,128)(2,1)S(1)} %bitcast.5), custom_call_target="tpu_custom_call" | custom-call | bytes 157286400 | tf_op jit(solution)/shard_map/middle/pallas_call | solution.py:672
  65.8 0.0 copy-start
  65.8 6.7 %apply_second.1 = (bf16[3,4,128,8,128]{4,3,2,1,0:T(8,128)(2,1)S(1)}, bf16[4,128,8,128]{3,2,1,0:T(8,128)(2,1)S(1)}, f32[4,8,128]{2,1,0:T(8,128)S(1)}) custom-call(s32[2,128]{1,0:T(2,128)S(1)} %bitcast.8, bf16[128,2,128,128]{3,2,1,0:T(8,128)(2,1)S(1)} %get-tuple-element.9.u_ref, bf16[384,32,128]{2,1,0:T(8,128)(2,1)S(1)} %bitcast.4, ...), custom_call_target="tpu_custom_call" | custom-call | flops 536870912 | bytes 8388608 | tf_op jit(solution)/shard_map/apply_second/pallas_call | solution.py:657
  72.5 0.0 copy-done
  72.6 30.8 %last.1 = (f32[8,16384]{1,0:T(8,128)S(1)}, f32[8,16384]{1,0:T(8,128)S(1)}) custom-call(bf16[3,4,128,8,128]{4,3,2,1,0:T(8,128)(2,1)S(1)} %get-tuple-element.13.part, f32[32,16384]{1,0:T(8,128)S(1)} %copy-done, bf16[4,128,8,128]{3,2,1,0:T(8,128)(2,1)S(1)} %get-tuple-element.14.h_ref, f32[4,8,128]{2,1,0:T(8,128)S(1)} %get-tuple-element.15.hq_ref), custom_call_target="tpu_custom_call" | custom-call | bytes 125829120 | tf_op jit(solution)/shard_map/last/pallas_call | solution.py:672
  103.4 0.8 copy.7
  104.2 0.8 copy.8
Async XLA Ops:
  0.6 19.0 %copy-start.1 = (s32[128,2]{0,1:T(2,128)S(1)}, s32[128,2]{0,1:T(2,128)}, u32[]{:S(2)}) copy-start(s32[128,2]{0,1:T(2,128)} %param.5) | copy-start | bytes 3076
  65.8 6.7 %copy-start = (f32[32,16384]{1,0:T(8,128)S(1)}, f32[32,16384]{1,0:T(8,128)}, u32[]{:S(2)}) copy-start(f32[32,16384]{1,0:T(8,128)} %p_ref.1) | copy-start | bytes 6291460

commit v7 on v6

--- a/solution.py
+++ b/solution.py
@@ -16,6 +16,7 @@
 ONES = 16
 UNROLL = 8
 ROW_UNROLL = 32
+PARTS = 2
 TRAFFIC = {"halo": 60 * MIB, "middle": 150 * MIB, "last": 120 * MIB}
 LIMITS = {"halo": 20 * MIB, "apply": 32 * MIB, "middle": 24 * MIB, "last": 24 * MIB}
 
@@ -29,12 +30,16 @@
     return lax.fori_loop(0, count, body, carry, unroll=unroll)
 
 
+def parts_of(split):
+    return [(k * (split // PARTS), split // PARTS) for k in range(PARTS)]
+
+
 def nothing():
     pass
 
 
 def low_of(count):
-    return count * 5 // 16 * 2
+    return count * 5 // (16 * PARTS) * 2 * PARTS
 
 
 class Place:
@@ -117,10 +122,18 @@
     split = low_of(count)
     low, high = pl.ds(0, split), pl.ds(split, count - split)
     order = (at.y, at.last_y, at.next_y, at.far_y)
-    own_high = Spread(at, window.at[0], split, count - split, send.at[0], recv.at[0])
-    next_low = Spread(at, window.at[2], 0, split, send.at[1], recv.at[1])
-    own_low = Spread(at, window.at[0], 0, split, send.at[2], recv.at[2])
-    x_low = remote(window.at[0, at.y, low], window.at[2, at.y, low], low_send, low_recv, at.behind)
+    own_high = Spread(at, window.at[0], split, count - split, send.at[2 * PARTS], recv.at[2 * PARTS])
+    next_low = [Spread(at, window.at[2], *part, send.at[k], recv.at[k]) for k, part in enumerate(parts_of(split))]
+    own_low = [
+        Spread(at, window.at[0], *part, send.at[PARTS + k], recv.at[PARTS + k])
+        for k, part in enumerate(parts_of(split))
+    ]
+    x_low = [
+        remote(
+            window.at[0, at.y, pl.ds(*part)], window.at[2, at.y, pl.ds(*part)], low_send.at[k], low_recv.at[k], at.behind
+        )
+        for k, part in enumerate(parts_of(split))
+    ]
     x_high = [
         remote(window.at[0, chunk, high], window.at[2, chunk, high], high_send.at[i], high_recv.at[i], at.behind)
         for i, chunk in enumerate(order)
@@ -137,38 +150,44 @@
     ]
     own_high.start()
     x_high[0].start()
+    for copy in x_low:
+        yield
+        copy.start()
     yield
-    x_low.start()
     own_high.relay()
     own_high.near()
     x_high[1].start()
     x_high[2].start()
-    own_low.start()
-    x_low.wait_recv()
-    next_low.start()
+    for k in range(PARTS):
+        x_low[k].wait_recv()
+        next_low[k].start()
+        if k:
+            next_low[k - 1].relay()
+        own_low[k].start()
+        if not k:
+            own_high.far()
+            x_high[3].start()
     across[0][0].start()
-    own_high.far()
-    x_high[3].start()
-    own_low.relay()
-    next_low.relay()
+    next_low[-1].relay()
+    for spread in own_low:
+        spread.relay()
     x_high[0].wait_recv()
     across[1][0].start()
-    next_low.near()
-    own_low.near()
+    for spread in next_low + own_low:
+        spread.near()
     across[0][1].start()
     across[0][2].start()
     for i in (1, 2):
         x_high[i].wait_recv()
         across[1][i].start()
-    next_low.far()
-    own_low.far()
+    for spread in next_low + own_low:
+        spread.far()
     across[0][3].start()
     x_high[3].wait_recv()
     across[1][3].start()
-    for spread in (own_high, next_low, own_low):
+    for spread in [own_high] + next_low + own_low:
         spread.drain()
-    x_low.wait_send()
-    for copy in x_high:
+    for copy in x_low + x_high:
         copy.wait_send()
     for copy in across[0] + across[1]:
         copy.wait()
@@ -263,15 +282,16 @@
 
 
 HALO_SEMS = pairs((2, 6), (2,), (4,), (4,))
-GATHER_SEMS = pairs((3, 6), (), (4,), (2, 4))
-REDUCE_SEMS = pairs((4,), (3, 6), (4,), ())
+GATHER_SEMS = pairs((2 * PARTS + 1, 6), (PARTS,), (4,), (2, 4))
+REDUCE_SEMS = pairs((4,), (2 * PARTS + 1, 6), (4,), (PARTS,))
 
 
 def reduce_scratch(blocks, sub, width):
+    most = max(low_of(blocks) // PARTS, blocks - low_of(blocks)) // 2
     return [
         pltpu.VMEM((RING, blocks, sub, width), BF16),
         pltpu.VMEM((2, RING, blocks, sub, width), BF16),
-        pltpu.VMEM((3, 6, low_of(blocks) // 2, sub, width), BF16),
+        pltpu.VMEM((2 * PARTS + 1, 6, most, sub, width), BF16),
         pltpu.VMEM((RING, blocks - low_of(blocks), sub, width), BF16),
         pltpu.VMEM((low_of(blocks), sub, width), BF16),
         pltpu.VMEM((low_of(blocks), sub, width), BF16),
@@ -356,9 +376,15 @@
         remote(part.at[1, chunk], crossed.at[chunk], c_send.at[i], c_recv.at[i], at.partner)
         for i, chunk in enumerate(order)
     ]
-    ahead_low = Fold(at, total.at[1], part.at[2], landed.at[0], 0, split, send.at[0], recv.at[0])
-    own_low = Fold(at, total.at[0], part.at[0], landed.at[1], 0, split, send.at[1], recv.at[1])
-    own_high = Fold(at, total.at[0], None, landed.at[2], split, high, send.at[2], recv.at[2])
+    parts = parts_of(split)
+    ahead_low, own_low = (
+        [
+            Fold(at, total.at[j], part.at[2 * j], landed.at[stream], *parts[k], send.at[stream], recv.at[stream])
+            for k, stream in enumerate(range(first, first + PARTS))
+        ]
+        for j, first in ((1, 0), (0, PARTS))
+    )
+    own_high = Fold(at, total.at[0], None, landed.at[2 * PARTS], split, high, send.at[2 * PARTS], recv.at[2 * PARTS])
     x_high, x_soon = (
         [
             remote(source.at[chunk, pl.ds(split, high)], behind.at[chunk], h_send.at[i], h_recv.at[i], at.ahead)
@@ -366,7 +392,10 @@
         ]
         for source in (total.at[1], part.at[2])
     )
-    x_low = remote(outgoing, incoming, low_send, low_recv, at.ahead)
+    x_low = [
+        remote(outgoing.at[pl.ds(*parts[k])], incoming.at[pl.ds(*parts[k])], low_send.at[k], low_recv.at[k], at.ahead)
+        for k in range(PARTS)
+    ]
     for copy in across:
         copy.start()
 
@@ -374,13 +403,15 @@
     def _():
         for copy in x_soon[:1]:
             copy.start()
-        ahead_low.begin()
+        for fold in ahead_low:
+            fold.begin()
         for copy in x_soon[1:]:
             copy.start()
 
     @pl.when(at.odd == 0)
     def _():
-        own_low.begin()
+        for fold in own_low:
+            fold.begin()
 
     def combine(index):
         chunk = order[index]
@@ -406,8 +437,11 @@
 
         loop(high, one)
 
-    def send_on(i, value):
-        outgoing[i] = value.astype(BF16)
+    def send_on(first, i, value):
+        outgoing[first + i] = value.astype(BF16)
+
+    def finish_low(first, i, value):
+        finish(first + i, 0.5 * (value + incoming[first + i].astype(F32)))
 
     for index in range(4):
         combine(index)
@@ -415,23 +449,24 @@
         @pl.when(at.odd == 0)
         def _(index=index):
             x_high[index].start()
-            if index < 3:
-                (ahead_low.far, ahead_low.next, ahead_low.last)[index]()
+            for fold in ahead_low if index < 3 else []:
+                (fold.far, fold.next, fold.last)[index]()
 
         @pl.when(at.odd == 1)
         def _(index=index):
-            if index < 3:
-                (own_low.far, own_low.next, own_low.last)[index]()
+            for fold in own_low if index < 3 else []:
+                (fold.far, fold.next, fold.last)[index]()
 
         if index == 0:
             beside[0]()
     beside[1]()
-    ahead_low.relay()
-    own_low.relay()
+    for fold in ahead_low + own_low:
+        fold.relay()
     join(0)
     own_high.far()
-    ahead_low.result(send_on)
-    x_low.start()
+    for k in range(PARTS):
+        ahead_low[k].result(functools.partial(send_on, parts[k][0]))
+        x_low[k].start()
     beside[2]()
     join(1)
     own_high.next()
@@ -443,13 +478,15 @@
     beside[4]()
     own_high.result(lambda i, value: finish(split + i, 0.5 * value))
     beside[5]()
-    x_low.wait_recv()
-    own_low.result(lambda i, value: finish(i, 0.5 * (value + incoming[i].astype(F32))))
+    for k in range(PARTS):
+        x_low[k].wait_recv()
+        own_low[k].result(functools.partial(finish_low, parts[k][0]))
+        beside[6]()
 
     def drain():
-        for copy in across + x_high + [x_low]:
+        for copy in across + x_high + x_low:
             copy.wait_send()
-        for fold in (ahead_low, own_low, own_high):
+        for fold in ahead_low + own_low + [own_high]:
             fold.drain()
 
     return drain
@@ -466,7 +503,7 @@
 
     count = 6 + len(REDUCE_SEMS)
     steps = gather(at, window, *scratch[count:])
-    drain = reduce(at, keep, [nothing] * 5 + [lambda: next(steps)], part, *scratch[:count])
+    drain = reduce(at, keep, [nothing] * 5 + [lambda: next(steps)] * 2, part, *scratch[:count])
     next(steps)
     drain()
 
@@ -559,7 +596,7 @@
         r_ref[:, pl.ds(pl.multiple_of(i * width, width), width)] = r_p * p_of(i) - r_h * h_of(i) + r_q * q
 
     tell(0)
-    drain = reduce(at, keep, [square, start_sums, pass_sums, nothing, end_sums, nothing], part, *scratch)
+    drain = reduce(at, keep, [square, start_sums, pass_sums, nothing, end_sums, nothing, nothing], part, *scratch)
     drain()
 
 

time: 105 us -> 107 us (1.019); the launches traced: 105 us -> 105 us
  no operation moved by 1% of the time
where the time goes in v7:
time: 107 us; the launch traced here: 105 us
  Pallas kernels  103 us (96%)
  local copies, waits for them, and re-layouts  1.6 us (1%)
    pallas_call x3, Pallas kernels, talk(): pl.pallas_call(body, out_shape=out_shape, in_specs=in_specs or [VMEM] * l...  90.1 us
    pallas_call x2, Pallas kernels, apply(): pl.pallas_call(functools.partial(apply_kernel, first), out_shape=out_shap...  13 us

profile of v7, /device:TPU:6, one launch (start us, length us, event | category | flops | bytes accessed | tf_op | source)
XLA Modules:
  0.0 105.4 jit_solution(4406241237451517422)
XLA Ops:
  0.6 0.0 copy-start.1
  0.6 19.0 %halo.1 = (bf16[3,4,32,32,128]{4,3,2,1,0:T(8,128)(2,1)S(1)}, bf16[128,2,128,128]{3,2,1,0:T(8,128)(2,1)S(1)}) custom-call(f32[32,16384]{1,0:T(8,128)} %p_ref.1, bf16[128,2,128,128]{3,2,1,0:T(8,128)(2,1)} %u_hbm.1), custom_call_target="tpu_custom_call" | custom-call | bytes 62914560 | tf_op jit(solution)/shard_map/halo/pallas_call | solution.py:709
  19.6 0.0 copy-done.1
  19.6 6.3 %apply_first.1 = (bf16[384,32,128]{2,1,0:T(8,128)(2,1)S(1)}, f32[384,8,128]{2,1,0:T(8,128)S(1)}) custom-call(s32[2,128]{1,0:T(2,128)S(1)} %bitcast.7, bf16[128,2,128,128]{3,2,1,0:T(8,128)(2,1)S(1)} %get-tuple-element.9.u_ref, bf16[384,32,128]{2,1,0:T(8,128)(2,1)S(1)} %bitcast.6), custom_call_target="tpu_custom_call" | custom-call | flops 536870912 | bytes 8388608 | tf_op jit(solution)/shard_map/apply_first/pallas_call | solution.py:694
  25.9 41.7 %middle.1 = bf16[3,4,32,32,128]{4,3,2,1,0:T(8,128)(2,1)S(1)} custom-call(bf16[3,4,32,32,128]{4,3,2,1,0:T(8,128)(2,1)S(1)} %bitcast.5), custom_call_target="tpu_custom_call" | custom-call | bytes 157286400 | tf_op jit(solution)/shard_map/middle/pallas_call | solution.py:709
  67.6 0.0 copy-start
  67.6 6.7 %apply_second.1 = (bf16[3,4,128,8,128]{4,3,2,1,0:T(8,128)(2,1)S(1)}, bf16[4,128,8,128]{3,2,1,0:T(8,128)(2,1)S(1)}, f32[4,8,128]{2,1,0:T(8,128)S(1)}) custom-call(s32[2,128]{1,0:T(2,128)S(1)} %bitcast.8, bf16[128,2,128,128]{3,2,1,0:T(8,128)(2,1)S(1)} %get-tuple-element.9.u_ref, bf16[384,32,128]{2,1,0:T(8,128)(2,1)S(1)} %bitcast.4, ...), custom_call_target="tpu_custom_call" | custom-call | flops 536870912 | bytes 8388608 | tf_op jit(solution)/shard_map/apply_second/pallas_call | solution.py:694
  74.4 0.0 copy-done
  74.4 29.4 %last.1 = (f32[8,16384]{1,0:T(8,128)S(1)}, f32[8,16384]{1,0:T(8,128)S(1)}) custom-call(bf16[3,4,128,8,128]{4,3,2,1,0:T(8,128)(2,1)S(1)} %get-tuple-element.13.part, f32[32,16384]{1,0:T(8,128)S(1)} %copy-done, bf16[4,128,8,128]{3,2,1,0:T(8,128)(2,1)S(1)} %get-tuple-element.14.h_ref, f32[4,8,128]{2,1,0:T(8,128)S(1)} %get-tuple-element.15.hq_ref), custom_call_target="tpu_custom_call" | custom-call | bytes 125829120 | tf_op jit(solution)/shard_map/last/pallas_call | solution.py:709
  103.8 0.8 copy.7
  104.6 0.8 copy.8
Async XLA Ops:
  0.6 19.0 %copy-start.1 = (s32[128,2]{0,1:T(2,128)S(1)}, s32[128,2]{0,1:T(2,128)}, u32[]{:S(2)}) copy-start(s32[128,2]{0,1:T(2,128)} %param.5) | copy-start | bytes 3076
  67.6 6.7 %copy-start = (f32[32,16384]{1,0:T(8,128)S(1)}, f32[32,16384]{1,0:T(8,128)}, u32[]{:S(2)}) copy-start(f32[32,16384]{1,0:T(8,128)} %p_ref.1) | copy-start | bytes 6291460

commit v8 on v6

--- a/solution.py
+++ b/solution.py
@@ -17,7 +17,7 @@
 UNROLL = 8
 ROW_UNROLL = 32
 TRAFFIC = {"halo": 60 * MIB, "middle": 150 * MIB, "last": 120 * MIB}
-LIMITS = {"halo": 20 * MIB, "apply": 32 * MIB, "middle": 24 * MIB, "last": 24 * MIB}
+LIMITS = {"halo": 20 * MIB, "apply": 26 * MIB, "middle": 30 * MIB, "last": 32 * MIB}
 
 
 def rem(value, count):
@@ -455,10 +455,35 @@
     return drain
 
 
-def middle_kernel(shards, part, window, *scratch):
+def terms(x_ref, back, along, deg, deg_along, take, dots=None):
+    rows, columns, width = along.shape
+    for d in (1, 0, 2):
+
+        def one(i, carry, d=d):
+            at_i = d * rows + i
+            weight, minus, x = deg[at_i], back[at_i], x_ref[at_i].astype(F32)
+            if d == 0:
+                weight += deg_along[i]
+                minus += along[i]
+            term = jnp.concatenate([weight] * (columns // 8), axis=0) * x - minus
+            take(d, i, x, term)
+            return carry if dots is None else carry + x * term
+
+        total = loop(rows, one, 0 if dots is None else dots)
+        dots = dots if dots is None else total
+    return dots
+
+
+def middle_kernel(shards, x_ref, back, along, deg, deg_along, window, part, *scratch):
     at = Place(shards)
     partners = (at.partner, at.ahead, at.behind, at.right, at.left)
     signal_all(partners)
+    quarter = window.shape[2]
+
+    def take(d, i, x, term):
+        part[d, i // quarter, rem(i, quarter)] = term.astype(BF16)
+
+    terms(x_ref, back, along, deg, deg_along, take)
     wait_all(partners)
 
     def keep(i, value):
@@ -471,14 +496,27 @@
     drain()
 
 
-def last_kernel(shards, groups, part, p_ref, h_ref, hq_ref, x_ref, r_ref, sums, heard, s_send, s_recv, *scratch):
+def last_kernel(
+    shards, groups, w_ref, back, along, deg, deg_along, p_ref, x_ref, r_ref,
+    part, h_ref, hq_ref, sums, heard, s_send, s_recv, *scratch,
+):
     at = Place(shards)
     opposite = (at.s, at.far_y)
     peers = [at.around(stride, size, step) for stride, size in groups for step in range(1, size)]
     partners = [at.partner, at.ahead, at.behind, at.right, at.left, opposite] + peers
     signal_all(partners)
+    _, blocks, sub, width = h_ref.shape
+
+    def take(d, i, x, term):
+        for g in range(RING):
+            part[d, g, i] = term[g * sub : (g + 1) * sub].astype(BF16)
+            if d == 0:
+                h_ref[g, i] = x[g * sub : (g + 1) * sub].astype(BF16)
+
+    dots = terms(w_ref, back, along, deg, deg_along, take, jnp.zeros((RING * sub, width), F32))
+    for g in range(RING):
+        hq_ref[g] = 0.5 * dots[g * sub : (g + 1) * sub]
     wait_all(partners)
-    _, blocks, sub, width = h_ref.shape
     zero = jnp.zeros((sub, width), F32)
     lanes = lax.broadcasted_iota(jnp.int32, (sub, width), 1)
     rounds = [[(hq_ref.at[y], at_y) for y, at_y in ((at.next_y, at.right), (at.last_y, at.left), (at.far_y, opposite))]]
@@ -563,15 +601,12 @@
     drain()
 
 
-def apply_kernel(first, nbr_ref, u_ref, x_ref, *rest):
-    if first:
-        part, deg, back, along, deg_along = rest
-    else:
-        deg, part, h_out, hq_out, back, along = rest
+def apply_kernel(first, nbr_ref, u_ref, x_ref, back, along, *weights):
     columns, width = x_ref.shape[1:]
     rows = u_ref.shape[0]
     base = lax.axis_index("rows") * rows
-    window = 3 * rows
+    if first:
+        deg, deg_along = weights
 
     def clear(i, carry):
         back[i] = jnp.zeros((columns, width), F32)
@@ -579,7 +614,7 @@
             deg[i] = jnp.zeros((8, width), F32)
         return carry
 
-    loop(window, clear)
+    loop(3 * rows, clear)
     ones = jnp.ones((ONES, 2 * width), BF16)
 
     def row(b, carry):
@@ -603,69 +638,26 @@
 
     lax.fori_loop(0, rows, row, 0, unroll=min(ROW_UNROLL, rows))
 
-    def term(i, own):
-        weight = deg[i]
-        minus = back[i]
-        if own:
-            minus += along[i]
-            if first:
-                weight += deg_along[i]
-                deg[i] = weight
-        x = x_ref[i].astype(F32)
-        return x, jnp.concatenate([weight] * (columns // 8), axis=0) * x - minus
-
-    dots = jnp.zeros((columns, width), F32)
-    for d in range(3):
-
-        def one(i, carry, d=d):
-            x, value = term(d * rows + i, d == 0)
-            carry += x * value
-            if first:
-                part[d * rows + i] = value.astype(BF16)
-            else:
-                for g in range(RING):
-                    at = slice(g * (columns // RING), (g + 1) * (columns // RING))
-                    part[d, g, i] = value[at].astype(BF16)
-                    if d == 0:
-                        h_out[g, i] = x[at].astype(BF16)
-            return carry
-
-        dots = loop(rows, one, dots)
-    if not first:
-        for g in range(RING):
-            hq_out[g] = 0.5 * dots[g * (columns // RING) : (g + 1) * (columns // RING)]
-
-
-def apply(first, nbr, upper, window, deg=None):
+
+def apply(first, nbr, upper, window):
     rows, slots, width, _ = upper.shape
     columns = window.shape[-2]
-    x = window.reshape(3 * rows, columns, width)
-    deg_shape = jax.ShapeDtypeStruct((3 * rows, 8, width), F32)
-    scratch = [pltpu.VMEM(x.shape, F32), pltpu.VMEM((rows, columns, width), F32)]
-    if first:
-        out_shape = [jax.ShapeDtypeStruct(x.shape, BF16), deg_shape]
-        scratch.append(pltpu.VMEM((rows, 8, width), F32))
-        args = (nbr, upper, x)
-    else:
-        sub = columns // RING
-        out_shape = [
-            jax.ShapeDtypeStruct((3, RING, rows, sub, width), BF16),
-            jax.ShapeDtypeStruct((RING, rows, sub, width), BF16),
-            jax.ShapeDtypeStruct((RING, sub, width), F32),
-        ]
-        args = (nbr, upper, x, deg)
+    out_shape = [
+        jax.ShapeDtypeStruct((count, lines, width), F32)
+        for lines in ((columns, 8) if first else (columns,))
+        for count in (3 * rows, rows)
+    ]
     return pl.pallas_call(
         functools.partial(apply_kernel, first),
         out_shape=out_shape,
-        in_specs=[pl.BlockSpec(memory_space=pltpu.SMEM)] + [VMEM] * (len(args) - 1),
+        in_specs=[pl.BlockSpec(memory_space=pltpu.SMEM), VMEM, VMEM],
         out_specs=[VMEM] * len(out_shape),
-        scratch_shapes=scratch,
         compiler_params=pltpu.CompilerParams(vmem_limit_bytes=LIMITS["apply"]),
         cost_estimate=pl.CostEstimate(
             flops=4 * rows * slots * width * width * columns, transcendentals=0, bytes_accessed=upper.size * 2
         ),
         name="apply_first" if first else "apply_second",
-    )(*args)
+    )(nbr, upper, window.reshape(3 * rows, columns, width))
 
 
 def talk(body, out_shape, scratch, collective_id, name, *args, in_specs=None):
@@ -705,29 +697,42 @@
         pltpu.with_memory_space_constraint(upper_blocks, pltpu.HBM),
         in_specs=[pl.BlockSpec(memory_space=pltpu.HBM)] * 2,
     )
-    part, deg = apply(True, nbr, upper, window)
+    flat = lambda w: w.reshape(3 * rows, columns, width)
+    back, along, deg, deg_along = apply(True, nbr, upper, window)
     window = talk(
         functools.partial(middle_kernel, shards),
         window_shape,
-        reduce_scratch(quarter, columns, width) + GATHER_SEMS,
+        [pltpu.VMEM(window_shape.shape, BF16)] + reduce_scratch(quarter, columns, width) + GATHER_SEMS,
         1,
         "middle",
-        part.reshape(window_shape.shape),
+        flat(window),
+        back,
+        along,
+        deg,
+        deg_along,
     )
-    part, h, hq = apply(False, nbr, upper, window, deg)
+    back, along = apply(False, nbr, upper, window)
     out_shape = jax.ShapeDtypeStruct((sub, rows * width), F32)
     return talk(
         functools.partial(last_kernel, shards, groups),
         (out_shape, out_shape),
-        [pltpu.VMEM((sub, width), F32), pltpu.VMEM((messages, sub, width), F32)]
+        [
+            pltpu.VMEM((3, RING, rows, sub, width), BF16),
+            pltpu.VMEM((RING, rows, sub, width), BF16),
+            pltpu.VMEM((RING, sub, width), F32),
+            pltpu.VMEM((sub, width), F32),
+            pltpu.VMEM((messages, sub, width), F32),
+        ]
         + pairs((messages,))
         + reduce_scratch(rows, sub, width),
         2,
         "last",
-        part,
+        flat(window),
+        back,
+        along,
+        deg,
+        deg_along,
         pass_rates,
-        h,
-        hq,
     )
 
 

time: 105 us -> 103 us (0.981)
  Pallas kernels: 103 us -> 100 us
    pallas_call x2, Pallas kernels: 13 us -> 10.1 us  [apply(): pl.pallas_call(functools.partial(apply_kernel, first), out_shape=out_shap...]
where the time goes in v8:
time: 103 us; the launch traced here: 102 us
  Pallas kernels  100 us (97%)
  local copies, waits for them, and re-layouts  1.6 us (2%)
    pallas_call x3, Pallas kernels, talk(): pl.pallas_call(body, out_shape=out_shape, in_specs=in_specs or [VMEM] * l...  89.8 us
    pallas_call x2, Pallas kernels, apply(): pl.pallas_call(functools.partial(apply_kernel, first), out_shape=out_shap...  10.1 us

profile of v8, /device:TPU:6, one launch (start us, length us, event | category | flops | bytes accessed | tf_op | source)
XLA Modules:
  0.0 102.3 jit_solution(3598246584575620086)
XLA Ops:
  0.6 0.0 copy-start.1
  0.6 19.0 %halo.1 = (bf16[3,4,32,32,128]{4,3,2,1,0:T(8,128)(2,1)S(1)}, bf16[128,2,128,128]{3,2,1,0:T(8,128)(2,1)S(1)}) custom-call(f32[32,16384]{1,0:T(8,128)} %p_ref.1, bf16[128,2,128,128]{3,2,1,0:T(8,128)(2,1)} %u_hbm.1), custom_call_target="tpu_custom_call" | custom-call | bytes 62914560 | tf_op jit(solution)/shard_map/halo/pallas_call | solution.py:664
  19.6 0.0 copy-done.1
  19.6 5.1 %apply_first.1 = (f32[384,32,128]{2,1,0:T(8,128)S(1)}, f32[128,32,128]{2,1,0:T(8,128)S(1)}, f32[384,8,128]{2,1,0:T(8,128)S(1)}, f32[128,8,128]{2,1,0:T(8,128)S(1)}) custom-call(s32[2,128]{1,0:T(2,128)S(1)} %bitcast.7, bf16[128,2,128,128]{3,2,1,0:T(8,128)(2,1)S(1)} %get-tuple-element.11.u_ref, bf16[384,32,128]{2,1,0:T(8,128)(2,1)S(1)} %bitcast.5), custom_call_target="tpu_custom_call" | custom-call | flops 536870912 | bytes 8388608 | tf_op jit(solution)/shard_map/apply_first/pallas_call | solution.py:650
  24.8 40.0 %middle.1 = bf16[3,4,32,32,128]{4,3,2,1,0:T(8,128)(2,1)S(1)} custom-call(bf16[384,32,128]{2,1,0:T(8,128)(2,1)S(1)} %bitcast.6, f32[384,32,128]{2,1,0:T(8,128)S(1)} %get-tuple-element.12.back, f32[128,32,128]{2,1,0:T(8,128)S(1)} %get-tuple-element.13.along, f32[384,8,128]{2,1,0:T(8,128)S(1)} %get-tuple-element.14.deg, ...), custom_call_target="tpu_custom_call" | custom-call | bytes 157286400 | tf_op jit(solution)/shard_map/middle/pallas_call | solution.py:664
  64.8 0.0 copy-start
  64.8 5.0 %apply_second.1 = (f32[384,32,128]{2,1,0:T(8,128)S(1)}, f32[128,32,128]{2,1,0:T(8,128)S(1)}) custom-call(s32[2,128]{1,0:T(2,128)S(1)} %bitcast.8, bf16[128,2,128,128]{3,2,1,0:T(8,128)(2,1)S(1)} %get-tuple-element.11.u_ref, bf16[384,32,128]{2,1,0:T(8,128)(2,1)S(1)} %bitcast.3), custom_call_target="tpu_custom_call" | custom-call | flops 536870912 | bytes 8388608 | tf_op jit(solution)/shard_map/apply_second/pallas_call | solution.py:650
  69.9 0.0 copy-done
  69.9 30.8 %last.1 = (f32[8,16384]{1,0:T(8,128)S(1)}, f32[8,16384]{1,0:T(8,128)S(1)}) custom-call(bf16[384,32,128]{2,1,0:T(8,128)(2,1)S(1)} %bitcast.4, f32[384,32,128]{2,1,0:T(8,128)S(1)} %get-tuple-element.16.back, f32[128,32,128]{2,1,0:T(8,128)S(1)} %get-tuple-element.17.along, f32[384,8,128]{2,1,0:T(8,128)S(1)} %get-tuple-element.14.deg, ...), custom_call_target="tpu_custom_call" | custom-call | bytes 125829120 | tf_op jit(solution)/shard_map/last/pallas_call | solution.py:664
  100.7 0.8 copy.7
  101.5 0.8 copy.8
Async XLA Ops:
  0.6 19.0 %copy-start.1 = (s32[128,2]{0,1:T(2,128)S(1)}, s32[128,2]{0,1:T(2,128)}, u32[]{:S(2)}) copy-start(s32[128,2]{0,1:T(2,128)} %param.5) | copy-start | bytes 3076
  64.8 5.0 %copy-start = (f32[32,16384]{1,0:T(8,128)S(1)}, f32[32,16384]{1,0:T(8,128)}, u32[]{:S(2)}) copy-start(f32[32,16384]{1,0:T(8,128)} %p_ref.1) | copy-start | bytes 6291460

commit v9 on v8

--- a/solution.py
+++ b/solution.py
@@ -15,7 +15,7 @@
 MIB = 2**20
 ONES = 16
 UNROLL = 8
-ROW_UNROLL = 32
+ROW_UNROLL = 128
 TRAFFIC = {"halo": 60 * MIB, "middle": 150 * MIB, "last": 120 * MIB}
 LIMITS = {"halo": 20 * MIB, "apply": 26 * MIB, "middle": 30 * MIB, "last": 32 * MIB}
 
@@ -344,7 +344,7 @@
 
 
 def reduce(
-    at, finish, beside,
+    at, finish, late, beside,
     part, crossed, total, landed, behind, outgoing, incoming,
     c_send, c_recv, send, recv, h_send, h_recv, low_send, low_recv,
 ):
@@ -370,6 +370,12 @@
     for copy in across:
         copy.start()
 
+    @pl.when(at.odd == 0)
+    def _():
+        own_low.begin()
+
+    late()
+
     @pl.when(at.odd == 1)
     def _():
         for copy in x_soon[:1]:
@@ -377,10 +383,6 @@
         ahead_low.begin()
         for copy in x_soon[1:]:
             copy.start()
-
-    @pl.when(at.odd == 0)
-    def _():
-        own_low.begin()
 
     def combine(index):
         chunk = order[index]
@@ -455,9 +457,9 @@
     return drain
 
 
-def terms(x_ref, back, along, deg, deg_along, take, dots=None):
+def terms(planes, x_ref, back, along, deg, deg_along, take, dots=None):
     rows, columns, width = along.shape
-    for d in (1, 0, 2):
+    for d in planes:
 
         def one(i, carry, d=d):
             at_i = d * rows + i
@@ -483,7 +485,8 @@
     def take(d, i, x, term):
         part[d, i // quarter, rem(i, quarter)] = term.astype(BF16)
 
-    terms(x_ref, back, along, deg, deg_along, take)
+    given = (x_ref, back, along, deg, deg_along, take)
+    terms((1, 0), *given)
     wait_all(partners)
 
     def keep(i, value):
@@ -491,7 +494,7 @@
 
     count = 6 + len(REDUCE_SEMS)
     steps = gather(at, window, *scratch[count:])
-    drain = reduce(at, keep, [nothing] * 5 + [lambda: next(steps)], part, *scratch[:count])
+    drain = reduce(at, keep, lambda: terms((2,), *given), [nothing] * 5 + [lambda: next(steps)], part, *scratch[:count])
     next(steps)
     drain()
 
@@ -513,9 +516,8 @@
             if d == 0:
                 h_ref[g, i] = x[g * sub : (g + 1) * sub].astype(BF16)
 
-    dots = terms(w_ref, back, along, deg, deg_along, take, jnp.zeros((RING * sub, width), F32))
-    for g in range(RING):
-        hq_ref[g] = 0.5 * dots[g * sub : (g + 1) * sub]
+    given = (w_ref, back, along, deg, deg_along, take)
+    dots = terms((1, 0), *given, jnp.zeros((RING * sub, width), F32))
     wait_all(partners)
     zero = jnp.zeros((sub, width), F32)
     lanes = lax.broadcasted_iota(jnp.int32, (sub, width), 1)
@@ -596,8 +598,13 @@
         r_p, r_h, r_q = scale
         r_ref[:, pl.ds(pl.multiple_of(i * width, width), width)] = r_p * p_of(i) - r_h * h_of(i) + r_q * q
 
-    tell(0)
-    drain = reduce(at, keep, [square, start_sums, pass_sums, nothing, end_sums, nothing], part, *scratch)
+    def late():
+        total = terms((2,), *given, dots)
+        for g in range(RING):
+            hq_ref[g] = 0.5 * total[g * sub : (g + 1) * sub]
+        tell(0)
+
+    drain = reduce(at, keep, late, [square, start_sums, pass_sums, nothing, end_sums, nothing], part, *scratch)
     drain()
 
 

time: 103 us -> 102 us (level); the launches traced: 102 us -> 102 us
  no operation moved by 1% of the time
where the time goes in v9:
time: 102 us
  Pallas kernels  100 us (98%)
  local copies, waits for them, and re-layouts  1.6 us (2%)
    pallas_call x3, Pallas kernels, talk(): pl.pallas_call(body, out_shape=out_shape, in_specs=in_specs or [VMEM] * l...  90.7 us
    pallas_call x2, Pallas kernels, apply(): pl.pallas_call(functools.partial(apply_kernel, first), out_shape=out_shap...  9.35 us

profile of v9, /device:TPU:6, one launch (start us, length us, event | category | flops | bytes accessed | tf_op | source)
XLA Modules:
  0.0 102.4 jit_solution(5514917820046237070)
XLA Ops:
  0.6 0.0 copy-start.1
  0.6 19.0 %halo.1 = (bf16[3,4,32,32,128]{4,3,2,1,0:T(8,128)(2,1)S(1)}, bf16[128,2,128,128]{3,2,1,0:T(8,128)(2,1)S(1)}) custom-call(f32[32,16384]{1,0:T(8,128)} %p_ref.1, bf16[128,2,128,128]{3,2,1,0:T(8,128)(2,1)} %u_hbm.1), custom_call_target="tpu_custom_call" | custom-call | bytes 62914560 | tf_op jit(solution)/shard_map/halo/pallas_call | solution.py:671
  19.6 0.0 copy-done.1
  19.6 4.7 %apply_first.1 = (f32[384,32,128]{2,1,0:T(8,128)S(1)}, f32[128,32,128]{2,1,0:T(8,128)S(1)}, f32[384,8,128]{2,1,0:T(8,128)S(1)}, f32[128,8,128]{2,1,0:T(8,128)S(1)}) custom-call(s32[2,128]{1,0:T(2,128)S(1)} %bitcast.7, bf16[128,2,128,128]{3,2,1,0:T(8,128)(2,1)S(1)} %get-tuple-element.11.u_ref, bf16[384,32,128]{2,1,0:T(8,128)(2,1)S(1)} %bitcast.5), custom_call_target="tpu_custom_call" | custom-call | flops 536870912 | bytes 8388608 | tf_op jit(solution)/shard_map/apply_first/pallas_call | solution.py:657
  24.4 40.5 %middle.1 = bf16[3,4,32,32,128]{4,3,2,1,0:T(8,128)(2,1)S(1)} custom-call(bf16[384,32,128]{2,1,0:T(8,128)(2,1)S(1)} %bitcast.6, f32[384,32,128]{2,1,0:T(8,128)S(1)} %get-tuple-element.12.back, f32[128,32,128]{2,1,0:T(8,128)S(1)} %get-tuple-element.13.along, f32[384,8,128]{2,1,0:T(8,128)S(1)} %get-tuple-element.14.deg, ...), custom_call_target="tpu_custom_call" | custom-call | bytes 157286400 | tf_op jit(solution)/shard_map/middle/pallas_call | solution.py:671
  64.9 0.0 copy-start
  64.9 4.6 %apply_second.1 = (f32[384,32,128]{2,1,0:T(8,128)S(1)}, f32[128,32,128]{2,1,0:T(8,128)S(1)}) custom-call(s32[2,128]{1,0:T(2,128)S(1)} %bitcast.8, bf16[128,2,128,128]{3,2,1,0:T(8,128)(2,1)S(1)} %get-tuple-element.11.u_ref, bf16[384,32,128]{2,1,0:T(8,128)(2,1)S(1)} %bitcast.3), custom_call_target="tpu_custom_call" | custom-call | flops 536870912 | bytes 8388608 | tf_op jit(solution)/shard_map/apply_second/pallas_call | solution.py:657
  69.5 0.0 copy-done
  69.5 31.2 %last.1 = (f32[8,16384]{1,0:T(8,128)S(1)}, f32[8,16384]{1,0:T(8,128)S(1)}) custom-call(bf16[384,32,128]{2,1,0:T(8,128)(2,1)S(1)} %bitcast.4, f32[384,32,128]{2,1,0:T(8,128)S(1)} %get-tuple-element.16.back, f32[128,32,128]{2,1,0:T(8,128)S(1)} %get-tuple-element.17.along, f32[384,8,128]{2,1,0:T(8,128)S(1)} %get-tuple-element.14.deg, ...), custom_call_target="tpu_custom_call" | custom-call | bytes 125829120 | tf_op jit(solution)/shard_map/last/pallas_call | solution.py:671
  100.8 0.8 copy.7
  101.6 0.8 copy.8
Async XLA Ops:
  0.6 19.0 %copy-start.1 = (s32[128,2]{0,1:T(2,128)S(1)}, s32[128,2]{0,1:T(2,128)}, u32[]{:S(2)}) copy-start(s32[128,2]{0,1:T(2,128)} %param.5) | copy-start | bytes 3076
  64.9 4.6 %copy-start = (f32[32,16384]{1,0:T(8,128)S(1)}, f32[32,16384]{1,0:T(8,128)}, u32[]{:S(2)}) copy-start(f32[32,16384]{1,0:T(8,128)} %p_ref.1) | copy-start | bytes 6291460

commit v10 on v9

--- a/solution.py
+++ b/solution.py
@@ -378,10 +378,8 @@
 
     @pl.when(at.odd == 1)
     def _():
-        for copy in x_soon[:1]:
-            copy.start()
         ahead_low.begin()
-        for copy in x_soon[1:]:
+        for copy in x_soon:
             copy.start()
 
     def combine(index):
@@ -416,9 +414,9 @@
 
         @pl.when(at.odd == 0)
         def _(index=index):
-            x_high[index].start()
             if index < 3:
                 (ahead_low.far, ahead_low.next, ahead_low.last)[index]()
+            x_high[index].start()
 
         @pl.when(at.odd == 1)
         def _(index=index):
@@ -427,9 +425,9 @@
 
         if index == 0:
             beside[0]()
-    beside[1]()
     ahead_low.relay()
     own_low.relay()
+    beside[1]()
     join(0)
     own_high.far()
     ahead_low.result(send_on)

time: 102 us -> 103 us (level)
  no operation moved by 1% of the time
where the time goes in v10:
time: 103 us
  Pallas kernels  100 us (97%)
  local copies, waits for them, and re-layouts  1.6 us (2%)
    pallas_call x3, Pallas kernels, talk(): pl.pallas_call(body, out_shape=out_shape, in_specs=in_specs or [VMEM] * l...  90.9 us
    pallas_call x2, Pallas kernels, apply(): pl.pallas_call(functools.partial(apply_kernel, first), out_shape=out_shap...  9.35 us

profile of v10, /device:TPU:6, one launch (start us, length us, event | category | flops | bytes accessed | tf_op | source)
XLA Modules:
  0.0 102.5 jit_solution(7741753579791140124)
XLA Ops:
  0.6 0.0 copy-start.1
  0.6 19.0 %halo.1 = (bf16[3,4,32,32,128]{4,3,2,1,0:T(8,128)(2,1)S(1)}, bf16[128,2,128,128]{3,2,1,0:T(8,128)(2,1)S(1)}) custom-call(f32[32,16384]{1,0:T(8,128)} %p_ref.1, bf16[128,2,128,128]{3,2,1,0:T(8,128)(2,1)} %u_hbm.1), custom_call_target="tpu_custom_call" | custom-call | bytes 62914560 | tf_op jit(solution)/shard_map/halo/pallas_call | solution.py:669
  19.6 0.0 copy-done.1
  19.6 4.7 %apply_first.1 = (f32[384,32,128]{2,1,0:T(8,128)S(1)}, f32[128,32,128]{2,1,0:T(8,128)S(1)}, f32[384,8,128]{2,1,0:T(8,128)S(1)}, f32[128,8,128]{2,1,0:T(8,128)S(1)}) custom-call(s32[2,128]{1,0:T(2,128)S(1)} %bitcast.7, bf16[128,2,128,128]{3,2,1,0:T(8,128)(2,1)S(1)} %get-tuple-element.11.u_ref, bf16[384,32,128]{2,1,0:T(8,128)(2,1)S(1)} %bitcast.5), custom_call_target="tpu_custom_call" | custom-call | flops 536870912 | bytes 8388608 | tf_op jit(solution)/shard_map/apply_first/pallas_call | solution.py:655
  24.4 40.5 %middle.1 = bf16[3,4,32,32,128]{4,3,2,1,0:T(8,128)(2,1)S(1)} custom-call(bf16[384,32,128]{2,1,0:T(8,128)(2,1)S(1)} %bitcast.6, f32[384,32,128]{2,1,0:T(8,128)S(1)} %get-tuple-element.12.back, f32[128,32,128]{2,1,0:T(8,128)S(1)} %get-tuple-element.13.along, f32[384,8,128]{2,1,0:T(8,128)S(1)} %get-tuple-element.14.deg, ...), custom_call_target="tpu_custom_call" | custom-call | bytes 157286400 | tf_op jit(solution)/shard_map/middle/pallas_call | solution.py:669
  64.9 0.0 copy-start
  64.9 4.6 %apply_second.1 = (f32[384,32,128]{2,1,0:T(8,128)S(1)}, f32[128,32,128]{2,1,0:T(8,128)S(1)}) custom-call(s32[2,128]{1,0:T(2,128)S(1)} %bitcast.8, bf16[128,2,128,128]{3,2,1,0:T(8,128)(2,1)S(1)} %get-tuple-element.11.u_ref, bf16[384,32,128]{2,1,0:T(8,128)(2,1)S(1)} %bitcast.3), custom_call_target="tpu_custom_call" | custom-call | flops 536870912 | bytes 8388608 | tf_op jit(solution)/shard_map/apply_second/pallas_call | solution.py:655
  69.6 0.0 copy-done
  69.6 31.3 %last.1 = (f32[8,16384]{1,0:T(8,128)S(1)}, f32[8,16384]{1,0:T(8,128)S(1)}) custom-call(bf16[384,32,128]{2,1,0:T(8,128)(2,1)S(1)} %bitcast.4, f32[384,32,128]{2,1,0:T(8,128)S(1)} %get-tuple-element.16.back, f32[128,32,128]{2,1,0:T(8,128)S(1)} %get-tuple-element.17.along, f32[384,8,128]{2,1,0:T(8,128)S(1)} %get-tuple-element.14.deg, ...), custom_call_target="tpu_custom_call" | custom-call | bytes 125829120 | tf_op jit(solution)/shard_map/last/pallas_call | solution.py:669
  100.9 0.8 copy.7
  101.7 0.8 copy.8
Async XLA Ops:
  0.6 19.0 %copy-start.1 = (s32[128,2]{0,1:T(2,128)S(1)}, s32[128,2]{0,1:T(2,128)}, u32[]{:S(2)}) copy-start(s32[128,2]{0,1:T(2,128)} %param.5) | copy-start | bytes 3076
  64.9 4.6 %copy-start = (f32[32,16384]{1,0:T(8,128)S(1)}, f32[32,16384]{1,0:T(8,128)}, u32[]{:S(2)}) copy-start(f32[32,16384]{1,0:T(8,128)} %p_ref.1) | copy-start | bytes 6291460
